TPU v7x, 256 devices: a whole 4x4x8 slice. The times are simulated.
256 devices in a mesh: sub: 256 (over z, y, x, core).
Axes of the slice: x: 4, y: 4, z: 8, core: 2. Of those that a mesh axis runs over, the one named last changes fastest.
Arguments:
- stiffness: float32 [256, 1024, 1024], P('sub'), as said below
- neumann_inv: float32 [256, 1024, 1024], P('sub'), as said below
- coarse_basis: float32 [256, 16, 1024], P('sub'), may hold values from -0.375 to 0.375
- coarse_inv: float32 [4096, 4096], P('sub'), as said below
- loads: float32 [256, 64, 1024], P('sub'), may hold values from -6 to 6
- face_index: int32 [256, 4, 128], P('sub'), may hold values from 0 to 1023, as said below
- face_len: int32 [256, 4], P('sub'), may hold values from 0 to 128, as said below
Outputs:
- solution: float32 [256, 64, 1024], P('sub')
- residual: float32 [256, 64, 1024], P('sub')
Inputs may be any that keep to these rules, and one draw needn't show every extreme that they name: `face_index`: within one subdomain all 512 entries are distinct. `face_len`: A block without a neighbour has length 0; paired blocks of two neighbours have equal length; some block has length 128. `stiffness`: each matrix is exactly symmetric and positive definite. `neumann_inv`: each matrix is exactly symmetric and positive definite. `coarse_inv`: the matrix is exactly symmetric and positive definite.
All inputs are finite; a program needn't handle non-finite values.
Results may differ from a plain program's by a relative error of at most 0.00022.
Values sent between devices are 32-bit elements; how exact they have to be, the bound alone decides.
A program may use at most 64 MiB of HBM per device.

v0:
```python
import jax
import jax.numpy as jnp
from jax import lax
from jax.sharding import PartitionSpec as P

CYCLE = 16
ITERS = 4


HIGH = lax.Precision.HIGHEST


def from_behind(value, axis, by):
    length = lax.axis_size(axis)
    pairs = [(i, i + by) for i in range(length) if 0 <= i + by < length]
    return lax.ppermute(value, axis, pairs)


def local(stiffness, neumann_inv, coarse_basis, coarse_inv, loads, face_index, face_len):
    stiff = stiffness[0]
    local_inv = neumann_inv[0]
    basis = coarse_basis[0]
    width = face_index.shape[2]
    face_slots = face_index[0].reshape(-1)
    slot_pos = jnp.arange(width, dtype=jnp.int32)
    live_slots = (slot_pos[None, :] < face_len[0][:, None]).astype(jnp.float32).reshape(-1)
    counts = jnp.ones((stiff.shape[0],), jnp.float32).at[face_slots].add(live_slots)
    weight = 1.0 / counts

    def assemble(local_vals):
        cases = local_vals.shape[0]
        face_vals = jnp.take(local_vals, face_slots, axis=1) * live_slots[None, :]
        blocks = face_vals.reshape(cases, 4, width)
        west_in = from_behind(blocks[:, 1], "sub", 1)
        east_in = from_behind(blocks[:, 0], "sub", -1)
        south_in = from_behind(blocks[:, 3], "sub", CYCLE)
        north_in = from_behind(blocks[:, 2], "sub", -CYCLE)
        incoming = jnp.stack([west_in, east_in, south_in, north_in], axis=1).reshape(cases, -1)
        incoming = incoming * live_slots[None, :]
        return local_vals.at[:, face_slots].add(incoming)

    def inner(left, right):
        return jnp.sum(left * right * weight[None, :], axis=1)

    def coarse_solve(coarse_res):
        return jnp.dot(
            coarse_inv, lax.all_gather(coarse_res, "sub", axis=0, tiled=True), precision=HIGH
        )

    def precond(resid):
        scaled = weight[None, :] * resid
        local_sol = jnp.dot(scaled, local_inv, precision=HIGH)
        coarse_res = jnp.einsum("cn,kn->ck", basis, scaled, precision=HIGH)
        coarse_sol = coarse_solve(coarse_res)
        local_sol = local_sol + jnp.einsum("ck,cn->kn", coarse_sol, basis, precision=HIGH)
        return assemble(weight[None, :] * local_sol)

    def progress_sum(resid, precond_res):
        return lax.psum(inner(resid, precond_res), "sub")

    residual = assemble(loads[0])
    solution = jnp.zeros_like(residual)
    precond_res = precond(residual)
    direction = precond_res
    rz_now = progress_sum(residual, precond_res)
    for step in range(ITERS):
        image = assemble(jnp.dot(direction, stiff, precision=HIGH))
        alpha = rz_now / lax.psum(inner(direction, image), "sub")
        solution = solution + alpha[:, None] * direction
        residual = residual - alpha[:, None] * image
        if step + 1 < ITERS:
            precond_res = precond(residual)
            rz_next = progress_sum(residual, precond_res)
            direction = precond_res + (rz_next / rz_now)[:, None] * direction
            rz_now = rz_next
    return (solution[None], residual[None])


def solution(mesh):
    placed = (
        P("sub", None, None),
        P("sub", None, None),
        P("sub", None, None),
        P("sub", None),
        P("sub", None, None),
        P("sub", None, None),
        P("sub", None),
    )
    return jax.shard_map(
        local,
        mesh=mesh,
        in_specs=placed,
        out_specs=(P("sub", None, None), P("sub", None, None)),
        check_vma=False,
    )
```

profile of v0, /device:TPU:1, one launch (start us, length us, event | category | flops | bytes accessed | tf_op | source)
XLA Modules:
  0.0 1297.2 jit_solution(2350251910647447329)
XLA Ops:
  17.6 5.5 collective-permute-start.2
  35.3 111.1 %all-gather.5.cloned.1.call-done = f32[4096,64]{1,0:T(8,128)} async-done(((f32[16,64]{1,0:T(8,128)}), f32[4096,64]{1,0:T(8,128)}) %all-gather.5.cloned.1.call-update) | async-done | bytes 1048592 | tf_op jit(solution)/shard_map/all_gather | solution.py:47
  146.4 5.0 fusion.88
  151.8 4.8 fusion.19
  162.7 5.5 collective-permute-start.6
  177.9 8.5 fusion.6
  190.9 6.0 collective-permute-start.10
  206.8 90.3 %all-reduce = (f32[64]{0:T(128)S(1)}, f32[64]{0:T(128)S(1)}) all-reduce(f32[64]{0:T(128)S(1)} %get-tuple-element.4, f32[64]{0:T(128)S(1)} %get-tuple-element.3), channel_id=1, replica_groups=mesh['sub'=256] {'sub'}, use_global_device_ids=true, to_apply=%region_4.6 | all-reduce | flops 128 | bytes 1024 | tf_op jit(solution)/shard_map/psum | solution.py:59
  298.4 100.4 %all-gather.7.cloned.1.call-done = f32[4096,64]{1,0:T(8,128)} async-done(((f32[16,64]{1,0:T(8,128)}), f32[4096,64]{1,0:T(8,128)}) %all-gather.7.cloned.1.call-update) | async-done | bytes 1048592 | tf_op jit(solution)/shard_map/all_gather | solution.py:47
  398.8 5.0 fusion.89
  404.1 4.8 fusion.25
  415.0 5.5 collective-permute-start.14
  430.1 83.8 %psum.58 = f32[64]{0:T(128)S(1)} all-reduce(f32[64]{0:T(128)S(1)} %multiply_reduce_fusion.5), channel_id=1, replica_groups=mesh['sub'=256] {'sub'}, use_global_device_ids=true, to_apply=%region_10.12 | all-reduce | flops 64 | bytes 512 | tf_op jit(solution)/shard_map/psum | solution.py:59
  514.0 8.5 fusion.4
  527.0 5.5 collective-permute-start.18
  542.1 85.6 %psum.59 = f32[64]{0:T(128)S(1)} all-reduce(f32[64]{0:T(128)S(1)} %multiply_reduce_fusion.4), channel_id=1, replica_groups=mesh['sub'=256] {'sub'}, use_global_device_ids=true, to_apply=%region_13.15 | all-reduce | flops 64 | bytes 512 | tf_op jit(solution)/shard_map/psum | solution.py:68
  629.1 100.3 %all-gather.9.cloned.1.call-done = f32[4096,64]{1,0:T(8,128)} async-done(((f32[16,64]{1,0:T(8,128)}), f32[4096,64]{1,0:T(8,128)}) %all-gather.9.cloned.1.call-update) | async-done | bytes 1048592 | tf_op jit(solution)/shard_map/all_gather | solution.py:47
  729.4 5.0 fusion.90
  734.8 4.8 fusion.31
  745.7 5.5 collective-permute-start.22
  760.8 84.0 %psum.60 = f32[64]{0:T(128)S(1)} all-reduce(f32[64]{0:T(128)S(1)} %multiply_reduce_fusion.3), channel_id=1, replica_groups=mesh['sub'=256] {'sub'}, use_global_device_ids=true, to_apply=%region_16.18 | all-reduce | flops 64 | bytes 512 | tf_op jit(solution)/shard_map/psum | solution.py:59
  844.9 8.5 fusion.2
  857.9 5.5 collective-permute-start.26
  873.0 85.8 %psum.61 = f32[64]{0:T(128)S(1)} all-reduce(f32[64]{0:T(128)S(1)} %multiply_reduce_fusion.2), channel_id=1, replica_groups=mesh['sub'=256] {'sub'}, use_global_device_ids=true, to_apply=%region_19.21 | all-reduce | flops 64 | bytes 512 | tf_op jit(solution)/shard_map/psum | solution.py:68
  959.8 100.6 %all-gather.11.cloned.1.call-done = f32[4096,64]{1,0:T(8,128)} async-done(((f32[16,64]{1,0:T(8,128)}), f32[4096,64]{1,0:T(8,128)}) %all-gather.11.cloned.1.call-update) | async-done | bytes 1048592 | tf_op jit(solution)/shard_map/all_gather | solution.py:47
  1060.5 5.0 fusion.91
  1065.8 4.8 fusion.37
  1076.7 5.5 collective-permute-start.30
  1091.8 83.8 %psum.62 = f32[64]{0:T(128)S(1)} all-reduce(f32[64]{0:T(128)S(1)} %multiply_reduce_fusion.1), channel_id=1, replica_groups=mesh['sub'=256] {'sub'}, use_global_device_ids=true, to_apply=%region_22.24 | all-reduce | flops 64 | bytes 512 | tf_op jit(solution)/shard_map/psum | solution.py:59
  1175.6 8.5 fusion
  1188.6 5.5 collective-permute-start.34
  1203.8 85.6 %psum.63 = f32[64]{0:T(128)S(1)} all-reduce(f32[64]{0:T(128)S(1)} %multiply_reduce_fusion), channel_id=1, replica_groups=mesh['sub'=256] {'sub'}, use_global_device_ids=true, to_apply=%region_25.27 | all-reduce | flops 64 | bytes 512 | tf_op jit(solution)/shard_map/psum | solution.py:68
  (178 shorter events, 147.3 us)
Async XLA Ops:
  7.2 139.2 %all-gather.5.cloned.1.call-start = ((), (), s32[]{:S(2)}) async-start(), calls=%async_computation | async-start | bytes 2105344 | tf_op jit(solution)/shard_map/all_gather | solution.py:47
  11.8 18.6 %collective-permute-start = (f32[64,128]{0,1:T(8,128)S(1)}, f32[64,128]{0,1:T(8,128)S(1)}, u32[]{:S(2)}, u32[]{:S(2)}) collective-permute-start(f32[64,128]{0,1:T(8,128)S(1)} %get-tuple-element.39), channel_id=1, source_target_pairs={{0,1},{1,2},{2,3},{3,4},{4,5},{5,6},{6,7},{7,8},{8,9},{9,10},{10,1... | collective-permute-start | bytes 98312 | tf_op jit(solution)/shard_map/ppermute | solution.py:16
  16.3 14.1 %collective-permute-start.3 = (f32[64,128]{0,1:T(8,128)S(1)}, f32[64,128]{0,1:T(8,128)S(1)}, u32[]{:S(2)}, u32[]{:S(2)}) collective-permute-start(f32[64,128]{0,1:T(8,128)S(1)} %get-tuple-element.40), channel_id=1, source_target_pairs={{16,0},{17,1},{18,2},{19,3},{20,4},{21,5},{22,6},{23,7},{24,8},{25... | collective-permute-start | bytes 98312 | tf_op jit(solution)/shard_map/ppermute | solution.py:16
  17.6 12.8 collective-permute-start.2
  23.1 7.3 collective-permute-start.1
  35.3 363.5 %all-gather.7.cloned.1.call-start = ((), (), s32[]{:S(2)}) async-start(), calls=%async_computation.1 | async-start | bytes 2105344 | tf_op jit(solution)/shard_map/all_gather | solution.py:47
  158.1 12.0 collective-permute-start.4
  161.4 8.7 collective-permute-start.7
  162.7 7.5 collective-permute-start.6
  187.7 12.2 collective-permute-start.8
  189.6 10.2 collective-permute-start.11
  190.9 9.0 collective-permute-start.10
  298.2 431.2 %all-gather.9.cloned.1.call-start = ((), (), s32[]{:S(2)}) async-start(), calls=%async_computation.2 | async-start | bytes 2105344 | tf_op jit(solution)/shard_map/all_gather | solution.py:47
  410.5 12.0 collective-permute-start.12
  413.7 8.7 collective-permute-start.15
  415.0 7.5 collective-permute-start.14
  523.8 11.7 collective-permute-start.16
  525.7 9.8 collective-permute-start.19
  527.0 8.5 collective-permute-start.18
  628.8 431.6 %all-gather.11.cloned.1.call-start = ((), (), s32[]{:S(2)}) async-start(), calls=%async_computation.3 | async-start | bytes 2105344 | tf_op jit(solution)/shard_map/all_gather | solution.py:47
  741.1 12.0 collective-permute-start.20
  744.4 8.7 collective-permute-start.23
  745.7 7.5 collective-permute-start.22
  854.7 11.7 collective-permute-start.24
  856.6 9.8 collective-permute-start.27
  857.9 8.5 collective-permute-start.26
  1072.1 12.0 collective-permute-start.28
  1075.4 8.7 collective-permute-start.31
  1076.7 7.5 collective-permute-start.30
  1185.4 11.7 collective-permute-start.32
  1187.3 9.8 collective-permute-start.35
  1188.6 8.5 collective-permute-start.34
  (10 other events, 211.3 us)
Sparse Core Ops, SparseCore 0:
  35.4 110.9 all-gather.4
  298.3 100.4 all-gather.6
  628.9 100.4 all-gather.8
  960.0 100.4 all-gather.10
where the time goes:
time: 1310 us; the launch traced here: 1300 us
  blocking collectives  599 us (46%)
  waiting for transfers between devices  438 us (33%)
  starting transfers between devices  109 us (8%)
  matrix products  78.4 us (6%)
  other arithmetic  44.7 us (3%)
  between operations  15.2 us (1%)
  local copies, waits for them, and re-layouts  13.1 us (1%)
    all_gather x4, waiting for transfers between devices, coarse_solve(): lax.all_gather(coarse_res, 'sub', axis=0, tiled=True)  412 us
    psum x4, blocking collectives, progress_sum(): return lax.psum(inner(resid, precond_res), 'sub')  342 us
    psum x3, blocking collectives, local(): alpha = rz_now / lax.psum(inner(direction, image), 'sub')  257 us
    ppermute x36, starting transfers between devices, from_behind(): return lax.ppermute(value, axis, pairs)  109 us
    dot_general x4, matrix products, local(): image = assemble(jnp.dot(direction, stiff, precision=HIGH))  34 us
    scatter-add x9, other arithmetic, assemble(): return local_vals.at[:, face_slots].add(incoming)  32.2 us
  transfers between devices with their start and end apart: 40, of which 12 were waited for; matrix products, arithmetic and copies ran while one was open for 0% of the time, Pallas kernels for 0%

commit v1 on v0

v1 whole, which is shorter than its diff:
```python
import functools

import jax
import jax.numpy as jnp
from jax import lax
from jax.experimental import pallas as pl
from jax.experimental.pallas import tpu as pltpu
from jax.sharding import PartitionSpec as P

CYCLE = 16
ITERS = 4
LINE = 8
ROWS = 4
MESH = pl.DeviceIdType.MESH
F32 = jnp.float32
BF16 = jnp.bfloat16


def halves(value):
    high = value.astype(BF16)
    return high, (value - high.astype(F32)).astype(BF16)


def thirds(value):
    high = value.astype(BF16)
    rest = value - high.astype(F32)
    mid = rest.astype(BF16)
    return high, mid, (rest - mid.astype(F32)).astype(BF16)


def dot(left, right):
    return jnp.dot(left, right, preferred_element_type=F32)


def dot_nt(left, right):
    return lax.dot_general(left, right, (((1,), (1,)), ((), ())), preferred_element_type=F32)


def iota(shape, dim):
    return lax.broadcasted_iota(jnp.int32, shape, dim)


def three(parts, cases):
    return parts[:cases] + parts[cases:2 * cases] + parts[2 * cases:]


def arrange(
    stiff_ref, neum_ref, basis_ref, loads_ref, index_ref,
    perm, neum_hi, neum_lo, stiff_hi, stiff_lo, basis_out, loads_out, turned_hi, turned_lo,
):
    cases, ndof = loads_ref.shape[1:]
    faces, width = index_ref.shape[1:]
    shared = faces * width

    columns = jnp.concatenate([index_ref[0].astype(F32), jnp.zeros((8 - faces, width), F32)], axis=0).T
    for block in range(faces):
        hit = columns[:, block:block + 1].astype(jnp.int32) == iota((width, ndof), 1)
        perm[block * width:(block + 1) * width, :] = jnp.where(hit, 1.0, 0.0).astype(BF16)
    taken = dot(jnp.ones((16, shared), BF16), perm[:shared, :])[:8]
    free = (1.0 - taken).astype(BF16)
    rank = jnp.zeros((8, ndof), F32)
    for block in range(0, ndof, 128):
        before = jnp.where(iota((128, ndof), 0) + block < iota((128, ndof), 1), 1.0, 0.0).astype(BF16)
        rank = rank + dot(free[:, block:block + 128], before)
    place = jnp.where(taken[:1] > 0.5, -1.0, rank[:1]).astype(jnp.int32)
    for block in range(0, ndof - shared, 128):
        hit = place == iota((128, ndof), 0) + block
        perm[shared + block:shared + block + 128, :] = jnp.where(hit, 1.0, 0.0).astype(BF16)

    loads_out[...] = three(dot_nt(jnp.concatenate(thirds(loads_ref[0]), axis=0), perm[...]), cases)
    basis = three(dot_nt(jnp.concatenate(thirds(basis_ref[0]), axis=0), perm[...]), 16)
    basis_hi, basis_lo = halves(basis)
    basis_out[...] = jnp.concatenate(
        [basis_hi, basis_lo, basis_hi, basis_lo, basis_hi, jnp.zeros_like(basis_hi)], axis=0
    )

    tall = 256
    for raw, out_hi, out_lo in ((neum_ref, neum_hi, neum_lo), (stiff_ref, stiff_hi, stiff_lo)):
        def turn(step, carry, raw=raw):
            here = pl.ds(pl.multiple_of(step * tall, tall), tall)
            high, low = halves(raw[0, here, :])
            both = dot_nt(jnp.concatenate([high, low], axis=0), perm[...]).astype(BF16)
            turned_hi[here, :] = both[:tall]
            turned_lo[here, :] = both[tall:]
            return carry

        def settle(step, carry, out_hi=out_hi, out_lo=out_lo):
            here = pl.ds(pl.multiple_of(step * tall, tall), tall)
            pick = perm[here, :]
            out_hi[here, :] = dot(pick, turned_hi[...]).astype(BF16)
            out_lo[here, :] = dot(pick, turned_lo[...]).astype(BF16)
            return carry

        lax.fori_loop(0, ndof // tall, turn, 0)
        lax.fori_loop(0, ndof // tall, settle, 0)


def restore(sol_ref, res_ref, perm, sol_out, res_out):
    cases = sol_ref.shape[0]
    sol_out[0] = three(dot(jnp.concatenate(thirds(sol_ref[...]), axis=0), perm[...]), cases)
    res_out[0] = three(dot(jnp.concatenate(thirds(res_ref[...]), axis=0), perm[...]), cases)


def kernel(
    sizes, cycle, neum_hi, neum_lo, stiff_hi, stiff_lo, basis, loads_ref, coarse_hbm, len_ref, sol_ref, res_ref,
    coarse_raw, coarse_cat, image_ref, direction_ref, local_ref, scalars, coarse_state, face_out, face_in,
    gather, gather_own, spread, spread_out, sums, sums_own, mids, mids_own, tops, tops_own,
    load_sem, face_send, face_recv, line_send, line_recv, rows_send, rows_recv, deep_send, deep_recv,
):
    planes, rows, line = sizes
    subs, plane = planes * rows * line, rows * line
    cases, ndof = loads_ref.shape
    faces, width = face_in.shape[1], face_in.shape[3]
    shared = faces * width
    wide = 2 * cases
    me = lax.axis_index("sub")
    deep, col = me // plane, lax.rem(me, plane)
    row, spot = col // line, lax.rem(col, line)
    left_half = iota((1, wide), 1) < cases

    def flip(value):
        return pltpu.roll(value, cases, axis=value.ndim - 1)

    sides = (
        lax.rem(me + subs - 1, subs), lax.rem(me + 1, subs),
        lax.rem(me + subs - cycle, subs), lax.rem(me + cycle, subs),
    )
    line_others = [(me - spot + at, at) for at in [lax.rem(spot + step, line) for step in range(1, line)]]
    rows_others = [(me + (at - row) * line, at) for at in [lax.rem(row + step, rows) for step in range(1, rows)]]
    deep_others = [(me + (at - deep) * plane, at) for at in [lax.rem(deep + step, planes) for step in range(1, planes)]]

    def remote(src, dst, send, recv, peer):
        return pltpu.make_async_remote_copy(
            src_ref=src, dst_ref=dst, send_sem=send, recv_sem=recv, device_id=(peer,), device_id_type=MESH
        )

    def coarse_cols(at):
        return pl.ds(pl.multiple_of(at * (plane * 16), plane * 16), plane * 16)

    load_coarse = pltpu.make_async_copy(coarse_hbm.at[:, coarse_cols(deep)], coarse_raw.at[deep], load_sem)
    load_coarse.start()

    barrier = pltpu.get_barrier_semaphore()
    everyone = [peer for peer, _ in line_others + rows_others + deep_others] + list(sides)
    for peer in everyone:
        pl.semaphore_signal(barrier, inc=1, device_id=(peer,), device_id_type=MESH)
    live = jnp.concatenate([iota((1, width), 1) < len_ref[0, block] for block in range(faces)], axis=1)
    weight = jnp.concatenate([jnp.where(live, 0.5, 1.0), jnp.ones((1, ndof - shared), F32)], axis=1)
    pl.semaphore_wait(barrier, len(everyone))

    def face_copy(kind, block):
        pair = block ^ 1
        return remote(
            face_out.at[kind, block], face_in.at[kind, pair], face_send.at[kind, block], face_recv.at[kind, pair],
            sides[block],
        )

    def start_faces(kind, value):
        for block in range(faces):
            face_out[kind, block] = value[:, block * width:(block + 1) * width]
        for block in range(faces):
            face_copy(kind, block).start()

    def wait_faces(kind):
        for block in range(faces):
            face_copy(kind, block).wait_send()
        for block in range(faces):
            face_copy(kind, block).wait_recv()
        got = jnp.concatenate([face_in[kind, block] for block in range(faces)], axis=1)
        return jnp.where(live, got, 0.0)

    def add_faces(value, incoming):
        return jnp.concatenate([value[:, :shared] + incoming, value[:, shared:]], axis=1)

    def product(value, mat_hi, mat_lo, start, stop):
        high, low = halves(value)
        first_part = dot(jnp.concatenate([high, low], axis=0), mat_hi[:, start:stop])
        return first_part[:cases] + first_part[cases:] + dot(high, mat_lo[:, start:stop])

    def push(kind, turn, others, src_of, dst, here, send, recv):
        return [
            remote(src_of(at), dst.at[turn, here], send.at[kind, turn, step], recv.at[kind, turn, here], peer)
            for step, (peer, at) in enumerate(others)
        ]

    def pull(kind, turn, others, src_of, dst, send, recv):
        return [
            remote(src_of(at), dst.at[turn, at], send.at[kind, turn, step], recv.at[kind, turn, at], peer)
            for step, (peer, at) in enumerate(others)
        ]

    def start_all(*args):
        for copy in push(*args):
            copy.start()

    def wait_all(kind, turn, others, src_of, dst, send, recv):
        for copy in pull(kind, turn, others, src_of, dst, send, recv):
            copy.wait_send()
        for copy in pull(kind, turn, others, src_of, dst, send, recv):
            copy.wait_recv()

    def start_gather(turn, field):
        high, low = halves(weight * field)
        out = dot_nt(basis[:32, :], jnp.concatenate([high, low], axis=0))
        value = out[:16] + flip(out[:16]) + out[16:]
        own = jnp.where(left_half, value[:8], flip(value[8:]))
        gather_own[...] = own
        gather[turn, row, spot] = own
        for step, (peer, at) in enumerate(line_others):
            remote(
                gather_own, gather.at[turn, row, spot], line_send.at[0, turn, step], line_recv.at[0, turn, spot], peer
            ).start()

    def pass_gather(turn):
        for receive in (False, True):
            for step, (peer, at) in enumerate(line_others):
                copy = remote(
                    gather_own, gather.at[turn, row, at], line_send.at[0, turn, step], line_recv.at[0, turn, at], peer
                )
                if receive:
                    copy.wait_recv()
                else:
                    copy.wait_send()
        start_all(0, turn, rows_others, lambda at: gather.at[turn, row], gather, row, rows_send, rows_recv)

    def start_spread(turn):
        wait_all(0, turn, rows_others, lambda at: gather.at[turn, row], gather, rows_send, rows_recv)
        packed = gather[turn].reshape(plane, 8, wide)
        turned = flip(packed)
        both = jnp.concatenate(
            [jnp.where(left_half, packed, turned), jnp.where(left_half, turned, packed)], axis=1
        ).reshape(plane * 16, wide)
        high = both.astype(BF16).astype(F32)
        right = jnp.where(left_half, high, both - high).astype(BF16)
        out = dot(coarse_cat[...], right)
        lines = planes * 16
        value = out[:lines] + flip(out[:lines]) + out[lines:]
        value = value.reshape(planes, 2, 8, wide)
        spread_out[...] = jnp.where(left_half, value[:, 0], flip(value[:, 1]))
        spread[turn, deep] = spread_out[deep]
        start_all(0, turn, deep_others, lambda at: spread_out.at[at], spread, deep, deep_send, deep_recv)

    def wait_spread(turn):
        wait_all(0, turn, deep_others, lambda at: spread_out.at[at], spread, deep_send, deep_recv)
        return jnp.sum(spread[turn], axis=0)

    def coarse_field(packed):
        both = jnp.concatenate([packed, flip(packed)], axis=0)
        high = both.astype(BF16).astype(F32)
        stacked = jnp.concatenate([high, high, both - high, jnp.zeros_like(high)], axis=0)
        return dot(stacked.T[:cases].astype(BF16), basis[32:, :])

    def row_sum(value):
        part = value[:, :128]
        for block in range(128, ndof, 128):
            part = part + value[:, block:block + 128]
        part = jnp.sum(part.T, axis=0, keepdims=True)
        return jnp.concatenate([part, part], axis=1)

    def as_column(scalar_row):
        return jnp.broadcast_to(scalar_row, (8, wide)).T[:cases, :1]

    def start_sums(turn, parts):
        own = jnp.concatenate(parts, axis=1)
        sums_own[...] = own
        sums[turn, spot] = own
        start_all(1, turn, line_others, lambda at: sums_own, sums, spot, line_send, line_recv)

    def pass_sums(turn):
        wait_all(1, turn, line_others, lambda at: sums_own, sums, line_send, line_recv)
        own = jnp.sum(sums[turn], axis=0)
        mids_own[...] = own
        mids[turn, row] = own
        start_all(1, turn, rows_others, lambda at: mids_own, mids, row, rows_send, rows_recv)

    def lift_sums(turn):
        wait_all(1, turn, rows_others, lambda at: mids_own, mids, rows_send, rows_recv)
        own = jnp.sum(mids[turn], axis=0)
        tops_own[...] = own
        tops[turn, deep] = own
        start_all(1, turn, deep_others, lambda at: tops_own, tops, deep, deep_send, deep_recv)

    def wait_sums(turn):
        wait_all(1, turn, deep_others, lambda at: tops_own, tops, deep_send, deep_recv)
        total = jnp.sum(tops[turn], axis=0)
        return total[:, :wide], total[:, wide:2 * wide], total[:, 2 * wide:]

    start_faces(1, loads_ref[...])
    for step, (peer, at) in enumerate(deep_others):
        remote(
            coarse_hbm.at[:, coarse_cols(at)], coarse_raw.at[deep], deep_send.at[2, 0, step], deep_recv.at[2, 0, deep], peer
        ).start()
    sol_ref[...] = jnp.zeros_like(sol_ref)
    direction_ref[...] = jnp.zeros_like(direction_ref)
    image_ref[...] = jnp.zeros_like(image_ref)
    scalars[...] = jnp.ones_like(scalars)
    resid = add_faces(loads_ref[...], wait_faces(1))
    start_gather(0, resid)
    res_ref[...] = resid
    load_coarse.wait()
    for receive in (False, True):
        for step, (peer, at) in enumerate(deep_others):
            copy = remote(
                coarse_hbm.at[:, coarse_cols(at)], coarse_raw.at[at], deep_send.at[2, 0, step], deep_recv.at[2, 0, at], peer
            )
            if receive:
                copy.wait_recv()
            else:
                copy.wait_send()
    coarse_hi, coarse_lo = halves(coarse_raw[...].reshape(planes * 16, plane * 16))
    coarse_cat[...] = jnp.concatenate([coarse_hi, coarse_lo], axis=0)
    pass_gather(0)
    local_ref[...] = product(weight * resid, neum_hi, neum_lo, 0, ndof)
    start_spread(0)
    coarse_state[0] = wait_spread(0)
    coarse_state[1] = jnp.zeros_like(coarse_state[1])

    def iterate(step, last):
        now, later = lax.rem(step, 2), lax.rem(step + 1, 2)
        half_sol = weight * (local_ref[...] + coarse_field(coarse_state[0]))
        start_faces(0, half_sol)
        rz_part = row_sum(half_sol * res_ref[...])
        precond = add_faces(half_sol, wait_faces(0))
        near = product(precond, stiff_hi, stiff_lo, 0, shared)
        start_faces(1, near)
        image = jnp.concatenate([near, product(precond, stiff_hi, stiff_lo, shared, ndof)], axis=1)
        zz_part = row_sum(precond * image)
        zq_part = row_sum(weight * precond * image_ref[...])
        start_sums(now, [rz_part, zz_part, zq_part])
        image = add_faces(image, wait_faces(1))
        if not last:
            start_gather(later, image)
        pass_sums(now)
        if not last:
            pass_gather(later)
        lift_sums(now)
        if not last:
            start_spread(later)
        rz, zz, zq = wait_sums(now)
        beta = jnp.where(step > 0, rz / scalars[0:1], 0.0)
        denom = zz + beta * (2.0 * zq) + beta * (beta * jnp.where(step > 0, scalars[1:2], 0.0))
        alpha = rz / denom
        slope, length = as_column(beta), as_column(alpha)
        direction = precond + slope * direction_ref[...]
        image = image + slope * image_ref[...]
        resid = res_ref[...] - length * image
        sol_ref[...] = sol_ref[...] + length * direction
        res_ref[...] = resid
        if not last:
            direction_ref[...] = direction
            image_ref[...] = image
            scalars[0:1] = rz
            scalars[1:2] = denom
            local_ref[...] = product(weight * resid, neum_hi, neum_lo, 0, ndof)
            coarse_image = wait_spread(later) + beta * coarse_state[1]
            coarse_state[1] = coarse_image
            coarse_state[0] = coarse_state[0] - alpha * coarse_image

    def body(step, carry):
        iterate(step, False)
        return carry

    lax.fori_loop(0, ITERS - 1, body, 0)
    iterate(jnp.int32(ITERS - 1), True)


def local(sizes, cycle, stiffness, neumann_inv, coarse_basis, coarse_inv, loads, face_index, face_len):
    cases, ndof = loads.shape[1:]
    faces, width = face_index.shape[1:]
    planes, rows, line = sizes
    plane = rows * line
    wide = 2 * cases
    anywhere = pl.BlockSpec(memory_space=pl.ANY)
    inside = pl.BlockSpec(memory_space=pltpu.VMEM)
    square = jax.ShapeDtypeStruct((ndof, ndof), BF16)
    plain = jax.ShapeDtypeStruct((cases, ndof), F32)
    whole = jax.ShapeDtypeStruct((1, cases, ndof), F32)
    roomy = 56 * 1024 * 1024

    perm, neum_hi, neum_lo, stiff_hi, stiff_lo, basis, fields = pl.pallas_call(
        arrange,
        out_shape=(square,) * 5 + (jax.ShapeDtypeStruct((96, ndof), BF16), plain),
        in_specs=[inside] * 5,
        out_specs=(inside,) * 7,
        scratch_shapes=[pltpu.VMEM((ndof, ndof), BF16)] * 2,
        compiler_params=pltpu.CompilerParams(vmem_limit_bytes=roomy),
        name="arrange",
    )(stiffness, neumann_inv, coarse_basis, loads, face_index)

    sol, res = pl.pallas_call(
        functools.partial(kernel, sizes, cycle),
        out_shape=(plain, plain),
        in_specs=[inside] * 6 + [anywhere, pl.BlockSpec(memory_space=pltpu.SMEM)],
        out_specs=(inside, inside),
        scratch_shapes=[
            pltpu.VMEM((planes, 16, plane * 16), F32),
            pltpu.VMEM((2 * planes * 16, plane * 16), BF16),
            pltpu.VMEM((cases, ndof), F32),
            pltpu.VMEM((cases, ndof), F32),
            pltpu.VMEM((cases, ndof), F32),
            pltpu.VMEM((8, wide), F32),
            pltpu.VMEM((2, 8, wide), F32),
            pltpu.VMEM((2, faces, cases, width), F32),
            pltpu.VMEM((2, faces, cases, width), F32),
            pltpu.VMEM((2, rows, line, 8, wide), F32),
            pltpu.VMEM((8, wide), F32),
            pltpu.VMEM((2, planes, 8, wide), F32),
            pltpu.VMEM((planes, 8, wide), F32),
            pltpu.VMEM((2, line, 1, 3 * wide), F32),
            pltpu.VMEM((1, 3 * wide), F32),
            pltpu.VMEM((2, rows, 1, 3 * wide), F32),
            pltpu.VMEM((1, 3 * wide), F32),
            pltpu.VMEM((2, planes, 1, 3 * wide), F32),
            pltpu.VMEM((1, 3 * wide), F32),
            pltpu.SemaphoreType.DMA,
            pltpu.SemaphoreType.DMA((2, faces)),
            pltpu.SemaphoreType.DMA((2, faces)),
            pltpu.SemaphoreType.DMA((2, 2, line)),
            pltpu.SemaphoreType.DMA((2, 2, line)),
            pltpu.SemaphoreType.DMA((2, 2, rows)),
            pltpu.SemaphoreType.DMA((2, 2, rows)),
            pltpu.SemaphoreType.DMA((3, 2, planes)),
            pltpu.SemaphoreType.DMA((3, 2, planes)),
        ],
        compiler_params=pltpu.CompilerParams(collective_id=0, has_side_effects=True, vmem_limit_bytes=roomy),
        name="solve",
    )(neum_hi, neum_lo, stiff_hi, stiff_lo, basis, fields, coarse_inv, face_len)

    return pl.pallas_call(
        restore,
        out_shape=(whole, whole),
        in_specs=[inside] * 3,
        out_specs=(inside, inside),
        compiler_params=pltpu.CompilerParams(vmem_limit_bytes=roomy),
        name="restore",
    )(sol, res, perm)


def solution(mesh, line=LINE, rows=ROWS, cycle=CYCLE):
    subs = mesh.shape["sub"]
    placed = (
        P("sub", None, None),
        P("sub", None, None),
        P("sub", None, None),
        P("sub", None),
        P("sub", None, None),
        P("sub", None, None),
        P("sub", None),
    )
    return jax.shard_map(
        functools.partial(local, (subs // (rows * line), rows, line), cycle),
        mesh=mesh,
        in_specs=placed,
        out_specs=(P("sub", None, None), P("sub", None, None)),
        check_vma=False,
    )
```

time: 1310 us -> 155 us (0.12)
  blocking collectives: 599 us -> 0 us
  waiting for transfers between devices: 438 us -> 0 us
  Pallas kernels: 0 us -> 153 us
  starting transfers between devices: 109 us -> 0 us
  matrix products: 78.4 us -> 0 us
  other arithmetic: 44.7 us -> 0 us
  between operations: 15.2 us -> 0.64 us
  local copies, waits for them, and re-layouts: 13.1 us -> 0 us
    psum x7 -> x0, blocking collectives: 599 us -> none  [the longest x4 342 us: progress_sum(): return lax.psum(inner(resid, precond_res), 'sub')]
    all_gather x4 -> x0, waiting for transfers between devices: 412 us -> none  [coarse_solve(): lax.all_gather(coarse_res, 'sub', axis=0, tiled=True)]
    pallas_call x0 -> x3, Pallas kernels: none -> 153 us  [the longest x1 121 us: local(): pl.pallas_call(functools.partial(kernel, sizes, cycle), out_shape=(plain,...]
    ppermute x36 -> x0, starting transfers between devices: 109 us -> none  [from_behind(): return lax.ppermute(value, axis, pairs)]
    dot_general x20 -> x0, matrix products: 78.4 us -> none  [the longest x4 34 us: local(): image = assemble(jnp.dot(direction, stiff, precision=HIGH))]
    scatter-add x10 -> x0, other arithmetic: 36.3 us -> none  [the longest x9 32.2 us: assemble(): return local_vals.at[:, face_slots].add(incoming)]
    ppermute x36 -> x0, waiting for transfers between devices: 25.2 us -> none  [from_behind(): return lax.ppermute(value, axis, pairs)]
  transfers between devices with their start and end apart: 40 -> 0, of which waited for: 12 -> 0; matrix products, arithmetic and copies ran while one was open for 0% -> 0% of each run, Pallas kernels for 0% -> 0%
where the time goes in v1:
time: 155 us; the launch traced here: 154 us
  Pallas kernels  153 us (99%)
    pallas_call x1, Pallas kernels, local(): pl.pallas_call(functools.partial(kernel, sizes, cycle), out_shape=(plain,...  121 us
    pallas_call x1, Pallas kernels, local(): pl.pallas_call(arrange, out_shape=(square,) * 5 + (jax.ShapeDtypeStruct((...  28.8 us
    pallas_call x1, Pallas kernels, local(): pl.pallas_call(restore, out_shape=(whole, whole), in_specs=[inside] * 3,...  3.48 us

profile of v1, /device:TPU:1, one launch (start us, length us, event | category | flops | bytes accessed | tf_op | source)
XLA Modules:
  0.0 154.0 jit_solution(7032238723213057102)
XLA Ops:
  0.6 28.8 %arrange.1 = (bf16[1024,1024]{1,0:T(8,128)(2,1)}, bf16[1024,1024]{1,0:T(8,128)(2,1)}, bf16[1024,1024]{1,0:T(8,128)(2,1)}, bf16[1024,1024]{1,0:T(8,128)(2,1)}, bf...) custom-call(f32[1,1024,1024]{2,1,0:T(8,128)} %stiff_ref.1, f32[1,1024,1024]{2,1,0:T(8,128)} %neum_ref.1, ...), custom_call_target="tpu_custom_call" | custom-call | tf_op jit(solution)/shard_map/arrange/pallas_call | solution.py:380
  29.5 121.0 %solve.1 = (f32[64,1024]{1,0:T(8,128)}, f32[64,1024]{1,0:T(8,128)}) custom-call(bf16[1024,1024]{1,0:T(8,128)(2,1)} %get-tuple-element.11.neum_hi, bf16[1024,1024]{1,0:T(8,128)(2,1)} %get-tuple-element.12.neum_lo, bf16[1024,1024]{1,0:T(8,128)(2,1)} %get-tuple-element.13.stiff_hi, bf16[1024,1024]{1,0:T(8,128)(2,1)} %get-tuple-element.14.stiff_lo, ...), custom_call_target="tpu_custom_call" | custom-call | tf_op jit(solution)/shard_map/solve/pallas_call | solution.py:390
  150.5 3.5 %restore.1 = (f32[1,64,1024]{2,1,0:T(8,128)}, f32[1,64,1024]{2,1,0:T(8,128)}) custom-call(f32[64,1024]{1,0:T(8,128)} %get-tuple-element.17.sol_ref, f32[64,1024]{1,0:T(8,128)} %get-tuple-element.18.res_ref, bf16[1024,1024]{1,0:T(8,128)(2,1)} %get-tuple-element.19.perm), custom_call_target="tpu_custom_call" | custom-call | tf_op jit(solution)/shard_map/restore/pallas_call | solution.py:429

commit v2 on v1

--- a/solution.py
+++ b/solution.py
@@ -44,72 +44,16 @@
     return parts[:cases] + parts[cases:2 * cases] + parts[2 * cases:]
 
 
-def arrange(
-    stiff_ref, neum_ref, basis_ref, loads_ref, index_ref,
-    perm, neum_hi, neum_lo, stiff_hi, stiff_lo, basis_out, loads_out, turned_hi, turned_lo,
-):
-    cases, ndof = loads_ref.shape[1:]
-    faces, width = index_ref.shape[1:]
-    shared = faces * width
-
-    columns = jnp.concatenate([index_ref[0].astype(F32), jnp.zeros((8 - faces, width), F32)], axis=0).T
-    for block in range(faces):
-        hit = columns[:, block:block + 1].astype(jnp.int32) == iota((width, ndof), 1)
-        perm[block * width:(block + 1) * width, :] = jnp.where(hit, 1.0, 0.0).astype(BF16)
-    taken = dot(jnp.ones((16, shared), BF16), perm[:shared, :])[:8]
-    free = (1.0 - taken).astype(BF16)
-    rank = jnp.zeros((8, ndof), F32)
-    for block in range(0, ndof, 128):
-        before = jnp.where(iota((128, ndof), 0) + block < iota((128, ndof), 1), 1.0, 0.0).astype(BF16)
-        rank = rank + dot(free[:, block:block + 128], before)
-    place = jnp.where(taken[:1] > 0.5, -1.0, rank[:1]).astype(jnp.int32)
-    for block in range(0, ndof - shared, 128):
-        hit = place == iota((128, ndof), 0) + block
-        perm[shared + block:shared + block + 128, :] = jnp.where(hit, 1.0, 0.0).astype(BF16)
-
-    loads_out[...] = three(dot_nt(jnp.concatenate(thirds(loads_ref[0]), axis=0), perm[...]), cases)
-    basis = three(dot_nt(jnp.concatenate(thirds(basis_ref[0]), axis=0), perm[...]), 16)
-    basis_hi, basis_lo = halves(basis)
-    basis_out[...] = jnp.concatenate(
-        [basis_hi, basis_lo, basis_hi, basis_lo, basis_hi, jnp.zeros_like(basis_hi)], axis=0
-    )
-
-    tall = 256
-    for raw, out_hi, out_lo in ((neum_ref, neum_hi, neum_lo), (stiff_ref, stiff_hi, stiff_lo)):
-        def turn(step, carry, raw=raw):
-            here = pl.ds(pl.multiple_of(step * tall, tall), tall)
-            high, low = halves(raw[0, here, :])
-            both = dot_nt(jnp.concatenate([high, low], axis=0), perm[...]).astype(BF16)
-            turned_hi[here, :] = both[:tall]
-            turned_lo[here, :] = both[tall:]
-            return carry
-
-        def settle(step, carry, out_hi=out_hi, out_lo=out_lo):
-            here = pl.ds(pl.multiple_of(step * tall, tall), tall)
-            pick = perm[here, :]
-            out_hi[here, :] = dot(pick, turned_hi[...]).astype(BF16)
-            out_lo[here, :] = dot(pick, turned_lo[...]).astype(BF16)
-            return carry
-
-        lax.fori_loop(0, ndof // tall, turn, 0)
-        lax.fori_loop(0, ndof // tall, settle, 0)
-
-
-def restore(sol_ref, res_ref, perm, sol_out, res_out):
-    cases = sol_ref.shape[0]
-    sol_out[0] = three(dot(jnp.concatenate(thirds(sol_ref[...]), axis=0), perm[...]), cases)
-    res_out[0] = three(dot(jnp.concatenate(thirds(res_ref[...]), axis=0), perm[...]), cases)
-
-
 def kernel(
-    sizes, cycle, neum_hi, neum_lo, stiff_hi, stiff_lo, basis, loads_ref, coarse_hbm, len_ref, sol_ref, res_ref,
+    sizes, cycle, stiff_hbm, neum_hbm, basis_ref, coarse_hbm, loads_ref, index_ref, len_ref, sol_out, res_out,
+    raw, perm, turned_hi, turned_lo, neum_hi, neum_lo, stiff_hi, stiff_lo, basis, sol_ref, res_ref,
     coarse_raw, coarse_cat, image_ref, direction_ref, local_ref, scalars, coarse_state, face_out, face_in,
     gather, gather_own, spread, spread_out, sums, sums_own, mids, mids_own, tops, tops_own,
     load_sem, face_send, face_recv, line_send, line_recv, rows_send, rows_recv, deep_send, deep_recv,
 ):
     planes, rows, line = sizes
     subs, plane = planes * rows * line, rows * line
-    cases, ndof = loads_ref.shape
+    cases, ndof = loads_ref.shape[1:]
     faces, width = face_in.shape[1], face_in.shape[3]
     shared = faces * width
     wide = 2 * cases
@@ -137,8 +81,12 @@
     def coarse_cols(at):
         return pl.ds(pl.multiple_of(at * (plane * 16), plane * 16), plane * 16)
 
-    load_coarse = pltpu.make_async_copy(coarse_hbm.at[:, coarse_cols(deep)], coarse_raw.at[deep], load_sem)
+    load_coarse = pltpu.make_async_copy(coarse_hbm.at[:, coarse_cols(deep)], coarse_raw.at[deep], load_sem.at[2])
+    load_neum = pltpu.make_async_copy(neum_hbm.at[0], raw.at[0], load_sem.at[0])
+    load_stiff = pltpu.make_async_copy(stiff_hbm.at[0], raw.at[1], load_sem.at[1])
+    load_neum.start()
     load_coarse.start()
+    load_stiff.start()
 
     barrier = pltpu.get_barrier_semaphore()
     everyone = [peer for peer, _ in line_others + rows_others + deep_others] + list(sides)
@@ -146,6 +94,13 @@
         pl.semaphore_signal(barrier, inc=1, device_id=(peer,), device_id_type=MESH)
     live = jnp.concatenate([iota((1, width), 1) < len_ref[0, block] for block in range(faces)], axis=1)
     weight = jnp.concatenate([jnp.where(live, 0.5, 1.0), jnp.ones((1, ndof - shared), F32)], axis=1)
+
+    columns = jnp.concatenate([index_ref[0].astype(F32), jnp.zeros((8 - faces, width), F32)], axis=0).T
+    for block in range(faces):
+        hit = columns[:, block:block + 1].astype(jnp.int32) == iota((width, ndof), 1)
+        perm[block * width:(block + 1) * width, :] = jnp.where(hit, 1.0, 0.0).astype(BF16)
+    loads_cat = jnp.concatenate(thirds(loads_ref[0]), axis=0)
+    first = three(dot_nt(loads_cat, perm[:shared, :]), cases)
     pl.semaphore_wait(barrier, len(everyone))
 
     def face_copy(kind, block):
@@ -285,7 +240,30 @@
         total = jnp.sum(tops[turn], axis=0)
         return total[:, :wide], total[:, wide:2 * wide], total[:, 2 * wide:]
 
-    start_faces(1, loads_ref[...])
+    tall = 256
+
+    def turn(which, start, stop):
+        def block(step, carry):
+            here = pl.ds(pl.multiple_of(step * tall, tall), tall)
+            high, low = halves(raw[which, here, :])
+            both = dot_nt(jnp.concatenate([high, low], axis=0), perm[start:stop, :]).astype(BF16)
+            turned_hi[here, start:stop] = both[:tall]
+            turned_lo[here, start:stop] = both[tall:]
+            return carry
+
+        lax.fori_loop(0, ndof // tall, block, 0)
+
+    def settle(out_hi, out_lo, start, stop, begin, end):
+        def block(step, carry):
+            here = pl.ds(pl.multiple_of(step * tall, tall), tall)
+            pick = perm[here, :]
+            out_hi[here, start:stop] = dot(pick, turned_hi[:, start:stop]).astype(BF16)
+            out_lo[here, start:stop] = dot(pick, turned_lo[:, start:stop]).astype(BF16)
+            return carry
+
+        lax.fori_loop(begin, end, block, 0)
+
+    start_faces(1, first)
     for step, (peer, at) in enumerate(deep_others):
         remote(
             coarse_hbm.at[:, coarse_cols(at)], coarse_raw.at[deep], deep_send.at[2, 0, step], deep_recv.at[2, 0, deep], peer
@@ -294,7 +272,25 @@
     direction_ref[...] = jnp.zeros_like(direction_ref)
     image_ref[...] = jnp.zeros_like(image_ref)
     scalars[...] = jnp.ones_like(scalars)
-    resid = add_faces(loads_ref[...], wait_faces(1))
+
+    taken = dot(jnp.ones((16, shared), BF16), perm[:shared, :])[:8]
+    free = (1.0 - taken).astype(BF16)
+    rank = jnp.zeros((8, ndof), F32)
+    for block in range(0, ndof, 128):
+        before = jnp.where(iota((128, ndof), 0) + block < iota((128, ndof), 1), 1.0, 0.0).astype(BF16)
+        rank = rank + dot(free[:, block:block + 128], before)
+    place = jnp.where(taken[:1] > 0.5, -1.0, rank[:1]).astype(jnp.int32)
+    for block in range(0, ndof - shared, 128):
+        hit = place == iota((128, ndof), 0) + block
+        perm[shared + block:shared + block + 128, :] = jnp.where(hit, 1.0, 0.0).astype(BF16)
+    rest = three(dot_nt(loads_cat, perm[shared:, :]), cases)
+    basis_hi, basis_lo = halves(three(dot_nt(jnp.concatenate(thirds(basis_ref[0]), axis=0), perm[...]), 16))
+    basis[...] = jnp.concatenate(
+        [basis_hi, basis_lo, basis_hi, basis_lo, basis_hi, jnp.zeros_like(basis_hi)], axis=0
+    )
+    load_neum.wait()
+    turn(0, 0, ndof)
+    resid = jnp.concatenate([first + wait_faces(1), rest], axis=1)
     start_gather(0, resid)
     res_ref[...] = resid
     load_coarse.wait()
@@ -309,20 +305,38 @@
                 copy.wait_send()
     coarse_hi, coarse_lo = halves(coarse_raw[...].reshape(planes * 16, plane * 16))
     coarse_cat[...] = jnp.concatenate([coarse_hi, coarse_lo], axis=0)
+    half_way = ndof // tall // 2
+    settle(neum_hi, neum_lo, 0, ndof, 0, half_way)
     pass_gather(0)
-    local_ref[...] = product(weight * resid, neum_hi, neum_lo, 0, ndof)
+    settle(neum_hi, neum_lo, 0, ndof, half_way, 2 * half_way)
     start_spread(0)
+    local_ref[...] = product(weight * res_ref[...], neum_hi, neum_lo, 0, ndof)
+    load_stiff.wait()
+    turn(1, 0, shared)
     coarse_state[0] = wait_spread(0)
     coarse_state[1] = jnp.zeros_like(coarse_state[1])
 
     def iterate(step, last):
-        now, later = lax.rem(step, 2), lax.rem(step + 1, 2)
+        now, later = (step % 2, (step + 1) % 2) if last else (lax.rem(step, 2), lax.rem(step + 1, 2))
         half_sol = weight * (local_ref[...] + coarse_field(coarse_state[0]))
         start_faces(0, half_sol)
         rz_part = row_sum(half_sol * res_ref[...])
+
+        if not last:
+            @pl.when(step == 0)
+            def _():
+                settle(stiff_hi, stiff_lo, 0, shared, 0, ndof // tall)
+
         precond = add_faces(half_sol, wait_faces(0))
         near = product(precond, stiff_hi, stiff_lo, 0, shared)
         start_faces(1, near)
+
+        if not last:
+            @pl.when(step == 0)
+            def _():
+                turn(1, shared, ndof)
+                settle(stiff_hi, stiff_lo, shared, ndof, 0, ndof // tall)
+
         image = jnp.concatenate([near, product(precond, stiff_hi, stiff_lo, shared, ndof)], axis=1)
         zz_part = row_sum(precond * image)
         zq_part = row_sum(weight * precond * image_ref[...])
@@ -361,7 +375,9 @@
         return carry
 
     lax.fori_loop(0, ITERS - 1, body, 0)
-    iterate(jnp.int32(ITERS - 1), True)
+    iterate(ITERS - 1, True)
+    sol_out[0] = three(dot(jnp.concatenate(thirds(sol_ref[...]), axis=0), perm[...]), cases)
+    res_out[0] = three(dot(jnp.concatenate(thirds(res_ref[...]), axis=0), perm[...]), cases)
 
 
 def local(sizes, cycle, stiffness, neumann_inv, coarse_basis, coarse_inv, loads, face_index, face_len):
@@ -372,27 +388,19 @@
     wide = 2 * cases
     anywhere = pl.BlockSpec(memory_space=pl.ANY)
     inside = pl.BlockSpec(memory_space=pltpu.VMEM)
-    square = jax.ShapeDtypeStruct((ndof, ndof), BF16)
-    plain = jax.ShapeDtypeStruct((cases, ndof), F32)
+    square = pltpu.VMEM((ndof, ndof), BF16)
+    plain = pltpu.VMEM((cases, ndof), F32)
     whole = jax.ShapeDtypeStruct((1, cases, ndof), F32)
-    roomy = 56 * 1024 * 1024
-
-    perm, neum_hi, neum_lo, stiff_hi, stiff_lo, basis, fields = pl.pallas_call(
-        arrange,
-        out_shape=(square,) * 5 + (jax.ShapeDtypeStruct((96, ndof), BF16), plain),
-        in_specs=[inside] * 5,
-        out_specs=(inside,) * 7,
-        scratch_shapes=[pltpu.VMEM((ndof, ndof), BF16)] * 2,
-        compiler_params=pltpu.CompilerParams(vmem_limit_bytes=roomy),
-        name="arrange",
-    )(stiffness, neumann_inv, coarse_basis, loads, face_index)
-
-    sol, res = pl.pallas_call(
+    return pl.pallas_call(
         functools.partial(kernel, sizes, cycle),
-        out_shape=(plain, plain),
-        in_specs=[inside] * 6 + [anywhere, pl.BlockSpec(memory_space=pltpu.SMEM)],
+        out_shape=(whole, whole),
+        in_specs=[anywhere, anywhere, inside, anywhere, inside, inside, pl.BlockSpec(memory_space=pltpu.SMEM)],
         out_specs=(inside, inside),
         scratch_shapes=[
+            pltpu.VMEM((2, ndof, ndof), F32),
+            square, square, square, square, square, square, square,
+            pltpu.VMEM((96, ndof), BF16),
+            plain, plain,
             pltpu.VMEM((planes, 16, plane * 16), F32),
             pltpu.VMEM((2 * planes * 16, plane * 16), BF16),
             pltpu.VMEM((cases, ndof), F32),
@@ -412,7 +420,7 @@
             pltpu.VMEM((1, 3 * wide), F32),
             pltpu.VMEM((2, planes, 1, 3 * wide), F32),
             pltpu.VMEM((1, 3 * wide), F32),
-            pltpu.SemaphoreType.DMA,
+            pltpu.SemaphoreType.DMA((3,)),
             pltpu.SemaphoreType.DMA((2, faces)),
             pltpu.SemaphoreType.DMA((2, faces)),
             pltpu.SemaphoreType.DMA((2, 2, line)),
@@ -422,18 +430,11 @@
             pltpu.SemaphoreType.DMA((3, 2, planes)),
             pltpu.SemaphoreType.DMA((3, 2, planes)),
         ],
-        compiler_params=pltpu.CompilerParams(collective_id=0, has_side_effects=True, vmem_limit_bytes=roomy),
+        compiler_params=pltpu.CompilerParams(
+            collective_id=0, has_side_effects=True, vmem_limit_bytes=56 * 1024 * 1024
+        ),
         name="solve",
-    )(neum_hi, neum_lo, stiff_hi, stiff_lo, basis, fields, coarse_inv, face_len)
-
-    return pl.pallas_call(
-        restore,
-        out_shape=(whole, whole),
-        in_specs=[inside] * 3,
-        out_specs=(inside, inside),
-        compiler_params=pltpu.CompilerParams(vmem_limit_bytes=roomy),
-        name="restore",
-    )(sol, res, perm)
+    )(stiffness, neumann_inv, coarse_basis, coarse_inv, loads, face_index, face_len)
 
 
 def solution(mesh, line=LINE, rows=ROWS, cycle=CYCLE):

time: 155 us -> 128 us (0.83)
  Pallas kernels: 153 us -> 122 us
  local copies, waits for them, and re-layouts: 0 us -> 3.34 us
    pallas_call x3 -> x1, Pallas kernels: 153 us -> 122 us  [local(): pl.pallas_call(functools.partial(kernel, sizes, cycle), out_shape=(whole,...]
    unnamed x0 -> x2, local copies, waits for them, and re-layouts: none -> 3.34 us
where the time goes in v2:
time: 128 us; the launch traced here: 126 us
  Pallas kernels  122 us (95%)
  local copies, waits for them, and re-layouts  3.34 us (3%)
    pallas_call x1, Pallas kernels, local(): pl.pallas_call(functools.partial(kernel, sizes, cycle), out_shape=(whole,...  122 us
    unnamed x2, local copies, waits for them, and re-layouts  3.34 us

profile of v2, /device:TPU:1, one launch (start us, length us, event | category | flops | bytes accessed | tf_op | source)
XLA Modules:
  0.0 126.0 jit_solution(701761257430286284)
XLA Ops:
  0.6 122.0 %solve.1 = (f32[1,64,1024]{2,1,0:T(8,128)}, f32[1,64,1024]{2,1,0:T(8,128)}) custom-call(f32[1,1024,1024]{2,1,0:T(8,128)} %stiff_hbm.1, f32[1,1024,1024]{2,1,0:T(8,128)} %neum_hbm.1, f32[1,16,1024]{2,1,0:T(8,128)} %basis_ref.1, f32[16,4096]{1,0:T(8,128)} %coarse_hbm.1, f32[1,64,1024]{2,1,0:T(8,128)} %loads_ref.1, s32[1,4,128]{2,1,0:T(4,128)} %index_ref.1, ...), custom_call_target="tpu_custom_call" | custom-call | tf_op jit(solution)/shard_map/solve/pallas_call | solution.py:394
  122.7 1.7 %copy.11 = f32[1,64,1024]{2,1,0:T(8,128)} copy(f32[1,64,1024]{2,1,0:T(8,128)} %get-tuple-element.4) | data formatting | bytes 524288
  124.3 1.7 %copy.12 = f32[1,64,1024]{2,1,0:T(8,128)} copy(f32[1,64,1024]{2,1,0:T(8,128)} %get-tuple-element.5) | data formatting | bytes 524288

commit v3 on v2

--- a/solution.py
+++ b/solution.py
@@ -9,8 +9,7 @@
 
 CYCLE = 16
 ITERS = 4
-LINE = 8
-ROWS = 4
+PLANE = 32
 MESH = pl.DeviceIdType.MESH
 F32 = jnp.float32
 BF16 = jnp.bfloat16
@@ -48,18 +47,17 @@
     sizes, cycle, stiff_hbm, neum_hbm, basis_ref, coarse_hbm, loads_ref, index_ref, len_ref, sol_out, res_out,
     raw, perm, turned_hi, turned_lo, neum_hi, neum_lo, stiff_hi, stiff_lo, basis, sol_ref, res_ref,
     coarse_raw, coarse_cat, image_ref, direction_ref, local_ref, scalars, coarse_state, face_out, face_in,
-    gather, gather_own, spread, spread_out, sums, sums_own, mids, mids_own, tops, tops_own,
-    load_sem, face_send, face_recv, line_send, line_recv, rows_send, rows_recv, deep_send, deep_recv,
+    gather, gather_own, spread, spread_out, sums, sums_own, tops, tops_own,
+    load_sem, face_send, face_recv, flat_send, flat_recv, deep_send, deep_recv,
 ):
-    planes, rows, line = sizes
-    subs, plane = planes * rows * line, rows * line
+    planes, plane = sizes
+    subs = planes * plane
     cases, ndof = loads_ref.shape[1:]
     faces, width = face_in.shape[1], face_in.shape[3]
     shared = faces * width
     wide = 2 * cases
     me = lax.axis_index("sub")
     deep, col = me // plane, lax.rem(me, plane)
-    row, spot = col // line, lax.rem(col, line)
     left_half = iota((1, wide), 1) < cases
 
     def flip(value):
@@ -69,8 +67,7 @@
         lax.rem(me + subs - 1, subs), lax.rem(me + 1, subs),
         lax.rem(me + subs - cycle, subs), lax.rem(me + cycle, subs),
     )
-    line_others = [(me - spot + at, at) for at in [lax.rem(spot + step, line) for step in range(1, line)]]
-    rows_others = [(me + (at - row) * line, at) for at in [lax.rem(row + step, rows) for step in range(1, rows)]]
+    flat_others = [(me - col + at, at) for at in [lax.rem(col + step, plane) for step in range(1, plane)]]
     deep_others = [(me + (at - deep) * plane, at) for at in [lax.rem(deep + step, planes) for step in range(1, planes)]]
 
     def remote(src, dst, send, recv, peer):
@@ -89,7 +86,7 @@
     load_stiff.start()
 
     barrier = pltpu.get_barrier_semaphore()
-    everyone = [peer for peer, _ in line_others + rows_others + deep_others] + list(sides)
+    everyone = [peer for peer, _ in flat_others + deep_others] + list(sides)
     for peer in everyone:
         pl.semaphore_signal(barrier, inc=1, device_id=(peer,), device_id_type=MESH)
     live = jnp.concatenate([iota((1, width), 1) < len_ref[0, block] for block in range(faces)], axis=1)
@@ -160,27 +157,12 @@
         value = out[:16] + flip(out[:16]) + out[16:]
         own = jnp.where(left_half, value[:8], flip(value[8:]))
         gather_own[...] = own
-        gather[turn, row, spot] = own
-        for step, (peer, at) in enumerate(line_others):
-            remote(
-                gather_own, gather.at[turn, row, spot], line_send.at[0, turn, step], line_recv.at[0, turn, spot], peer
-            ).start()
-
-    def pass_gather(turn):
-        for receive in (False, True):
-            for step, (peer, at) in enumerate(line_others):
-                copy = remote(
-                    gather_own, gather.at[turn, row, at], line_send.at[0, turn, step], line_recv.at[0, turn, at], peer
-                )
-                if receive:
-                    copy.wait_recv()
-                else:
-                    copy.wait_send()
-        start_all(0, turn, rows_others, lambda at: gather.at[turn, row], gather, row, rows_send, rows_recv)
+        gather[turn, col] = own
+        start_all(0, turn, flat_others, lambda at: gather_own, gather, col, flat_send, flat_recv)
 
     def start_spread(turn):
-        wait_all(0, turn, rows_others, lambda at: gather.at[turn, row], gather, rows_send, rows_recv)
-        packed = gather[turn].reshape(plane, 8, wide)
+        wait_all(0, turn, flat_others, lambda at: gather_own, gather, flat_send, flat_recv)
+        packed = gather[turn]
         turned = flip(packed)
         both = jnp.concatenate(
             [jnp.where(left_half, packed, turned), jnp.where(left_half, turned, packed)], axis=1
@@ -218,19 +200,12 @@
     def start_sums(turn, parts):
         own = jnp.concatenate(parts, axis=1)
         sums_own[...] = own
-        sums[turn, spot] = own
-        start_all(1, turn, line_others, lambda at: sums_own, sums, spot, line_send, line_recv)
-
-    def pass_sums(turn):
-        wait_all(1, turn, line_others, lambda at: sums_own, sums, line_send, line_recv)
+        sums[turn, col] = own
+        start_all(1, turn, flat_others, lambda at: sums_own, sums, col, flat_send, flat_recv)
+
+    def lift_sums(turn):
+        wait_all(1, turn, flat_others, lambda at: sums_own, sums, flat_send, flat_recv)
         own = jnp.sum(sums[turn], axis=0)
-        mids_own[...] = own
-        mids[turn, row] = own
-        start_all(1, turn, rows_others, lambda at: mids_own, mids, row, rows_send, rows_recv)
-
-    def lift_sums(turn):
-        wait_all(1, turn, rows_others, lambda at: mids_own, mids, rows_send, rows_recv)
-        own = jnp.sum(mids[turn], axis=0)
         tops_own[...] = own
         tops[turn, deep] = own
         start_all(1, turn, deep_others, lambda at: tops_own, tops, deep, deep_send, deep_recv)
@@ -305,10 +280,7 @@
                 copy.wait_send()
     coarse_hi, coarse_lo = halves(coarse_raw[...].reshape(planes * 16, plane * 16))
     coarse_cat[...] = jnp.concatenate([coarse_hi, coarse_lo], axis=0)
-    half_way = ndof // tall // 2
-    settle(neum_hi, neum_lo, 0, ndof, 0, half_way)
-    pass_gather(0)
-    settle(neum_hi, neum_lo, 0, ndof, half_way, 2 * half_way)
+    settle(neum_hi, neum_lo, 0, ndof, 0, ndof // tall)
     start_spread(0)
     local_ref[...] = product(weight * res_ref[...], neum_hi, neum_lo, 0, ndof)
     load_stiff.wait()
@@ -344,9 +316,6 @@
         image = add_faces(image, wait_faces(1))
         if not last:
             start_gather(later, image)
-        pass_sums(now)
-        if not last:
-            pass_gather(later)
         lift_sums(now)
         if not last:
             start_spread(later)
@@ -383,8 +352,7 @@
 def local(sizes, cycle, stiffness, neumann_inv, coarse_basis, coarse_inv, loads, face_index, face_len):
     cases, ndof = loads.shape[1:]
     faces, width = face_index.shape[1:]
-    planes, rows, line = sizes
-    plane = rows * line
+    planes, plane = sizes
     wide = 2 * cases
     anywhere = pl.BlockSpec(memory_space=pl.ANY)
     inside = pl.BlockSpec(memory_space=pltpu.VMEM)
@@ -410,23 +378,19 @@
             pltpu.VMEM((2, 8, wide), F32),
             pltpu.VMEM((2, faces, cases, width), F32),
             pltpu.VMEM((2, faces, cases, width), F32),
-            pltpu.VMEM((2, rows, line, 8, wide), F32),
+            pltpu.VMEM((2, plane, 8, wide), F32),
             pltpu.VMEM((8, wide), F32),
             pltpu.VMEM((2, planes, 8, wide), F32),
             pltpu.VMEM((planes, 8, wide), F32),
-            pltpu.VMEM((2, line, 1, 3 * wide), F32),
-            pltpu.VMEM((1, 3 * wide), F32),
-            pltpu.VMEM((2, rows, 1, 3 * wide), F32),
+            pltpu.VMEM((2, plane, 1, 3 * wide), F32),
             pltpu.VMEM((1, 3 * wide), F32),
             pltpu.VMEM((2, planes, 1, 3 * wide), F32),
             pltpu.VMEM((1, 3 * wide), F32),
             pltpu.SemaphoreType.DMA((3,)),
             pltpu.SemaphoreType.DMA((2, faces)),
             pltpu.SemaphoreType.DMA((2, faces)),
-            pltpu.SemaphoreType.DMA((2, 2, line)),
-            pltpu.SemaphoreType.DMA((2, 2, line)),
-            pltpu.SemaphoreType.DMA((2, 2, rows)),
-            pltpu.SemaphoreType.DMA((2, 2, rows)),
+            pltpu.SemaphoreType.DMA((2, 2, plane)),
+            pltpu.SemaphoreType.DMA((2, 2, plane)),
             pltpu.SemaphoreType.DMA((3, 2, planes)),
             pltpu.SemaphoreType.DMA((3, 2, planes)),
         ],
@@ -437,7 +401,7 @@
     )(stiffness, neumann_inv, coarse_basis, coarse_inv, loads, face_index, face_len)
 
 
-def solution(mesh, line=LINE, rows=ROWS, cycle=CYCLE):
+def solution(mesh, plane=PLANE, cycle=CYCLE):
     subs = mesh.shape["sub"]
     placed = (
         P("sub", None, None),
@@ -449,7 +413,7 @@
         P("sub", None),
     )
     return jax.shard_map(
-        functools.partial(local, (subs // (rows * line), rows, line), cycle),
+        functools.partial(local, (subs // plane, plane), cycle),
         mesh=mesh,
         in_specs=placed,
         out_specs=(P("sub", None, None), P("sub", None, None)),

time: 128 us -> 118 us (0.922); the launches traced: 126 us -> 118 us
  Pallas kernels: 122 us -> 114 us
    pallas_call x1, Pallas kernels: 122 us -> 114 us  [local(): pl.pallas_call(functools.partial(kernel, sizes, cycle), out_shape=(whole,...]
where the time goes in v3:
time: 118 us
  Pallas kernels  114 us (97%)
  local copies, waits for them, and re-layouts  3.34 us (3%)
    pallas_call x1, Pallas kernels, local(): pl.pallas_call(functools.partial(kernel, sizes, cycle), out_shape=(whole,...  114 us
    unnamed x2, local copies, waits for them, and re-layouts  3.34 us

profile of v3, /device:TPU:1, one launch (start us, length us, event | category | flops | bytes accessed | tf_op | source)
XLA Modules:
  0.0 117.9 jit_solution(4490177053586605684)
XLA Ops:
  0.6 113.9 %solve.1 = (f32[1,64,1024]{2,1,0:T(8,128)}, f32[1,64,1024]{2,1,0:T(8,128)}) custom-call(f32[1,1024,1024]{2,1,0:T(8,128)} %stiff_hbm.1, f32[1,1024,1024]{2,1,0:T(8,128)} %neum_hbm.1, f32[1,16,1024]{2,1,0:T(8,128)} %basis_ref.1, f32[16,4096]{1,0:T(8,128)} %coarse_hbm.1, f32[1,64,1024]{2,1,0:T(8,128)} %loads_ref.1, s32[1,4,128]{2,1,0:T(4,128)} %index_ref.1, ...), custom_call_target="tpu_custom_call" | custom-call | tf_op jit(solution)/shard_map/solve/pallas_call | solution.py:362
  114.5 1.7 %copy.11 = f32[1,64,1024]{2,1,0:T(8,128)} copy(f32[1,64,1024]{2,1,0:T(8,128)} %get-tuple-element.4) | data formatting | bytes 524288
  116.2 1.7 %copy.12 = f32[1,64,1024]{2,1,0:T(8,128)} copy(f32[1,64,1024]{2,1,0:T(8,128)} %get-tuple-element.5) | data formatting | bytes 524288

commit v4 on v3

--- a/solution.py
+++ b/solution.py
@@ -151,9 +151,11 @@
         for copy in pull(kind, turn, others, src_of, dst, send, recv):
             copy.wait_recv()
 
-    def start_gather(turn, field):
-        high, low = halves(weight * field)
-        out = dot_nt(basis[:32, :], jnp.concatenate([high, low], axis=0))
+    def coarse_of(scaled):
+        high, low = halves(scaled)
+        return dot_nt(basis[:32, :scaled.shape[1]], jnp.concatenate([high, low], axis=0))
+
+    def start_gather(turn, out):
         value = out[:16] + flip(out[:16]) + out[16:]
         own = jnp.where(left_half, value[:8], flip(value[8:]))
         gather_own[...] = own
@@ -181,11 +183,11 @@
         wait_all(0, turn, deep_others, lambda at: spread_out.at[at], spread, deep_send, deep_recv)
         return jnp.sum(spread[turn], axis=0)
 
-    def coarse_field(packed):
+    def coarse_rows(packed):
         both = jnp.concatenate([packed, flip(packed)], axis=0)
         high = both.astype(BF16).astype(F32)
         stacked = jnp.concatenate([high, high, both - high, jnp.zeros_like(high)], axis=0)
-        return dot(stacked.T[:cases].astype(BF16), basis[32:, :])
+        return stacked.T[:cases].astype(BF16)
 
     def row_sum(value):
         part = value[:, :128]
@@ -264,9 +266,9 @@
         [basis_hi, basis_lo, basis_hi, basis_lo, basis_hi, jnp.zeros_like(basis_hi)], axis=0
     )
     load_neum.wait()
-    turn(0, 0, ndof)
+    turn(0, 0, shared)
     resid = jnp.concatenate([first + wait_faces(1), rest], axis=1)
-    start_gather(0, resid)
+    start_gather(0, coarse_of(weight * resid))
     res_ref[...] = resid
     load_coarse.wait()
     for receive in (False, True):
@@ -280,23 +282,31 @@
                 copy.wait_send()
     coarse_hi, coarse_lo = halves(coarse_raw[...].reshape(planes * 16, plane * 16))
     coarse_cat[...] = jnp.concatenate([coarse_hi, coarse_lo], axis=0)
-    settle(neum_hi, neum_lo, 0, ndof, 0, ndof // tall)
+    turn(0, shared, ndof)
+    settle(neum_hi, neum_lo, 0, shared, 0, ndof // tall)
     start_spread(0)
+    settle(neum_hi, neum_lo, shared, ndof, 0, ndof // tall)
     local_ref[...] = product(weight * res_ref[...], neum_hi, neum_lo, 0, ndof)
     load_stiff.wait()
-    turn(1, 0, shared)
     coarse_state[0] = wait_spread(0)
     coarse_state[1] = jnp.zeros_like(coarse_state[1])
 
+    def unturn(one, two):
+        both = three(dot(jnp.concatenate(thirds(jnp.concatenate([one, two], axis=0)), axis=0), perm[...]), 2 * cases)
+        return [both[:cases], both[cases:]]
+
     def iterate(step, last):
         now, later = (step % 2, (step + 1) % 2) if last else (lax.rem(step, 2), lax.rem(step + 1, 2))
-        half_sol = weight * (local_ref[...] + coarse_field(coarse_state[0]))
-        start_faces(0, half_sol)
+        coarse_part = coarse_rows(coarse_state[0])
+        near_sol = weight[:, :shared] * (local_ref[:, :shared] + dot(coarse_part, basis[32:, :shared]))
+        start_faces(0, near_sol)
+        half_sol = jnp.concatenate([near_sol, local_ref[:, shared:] + dot(coarse_part, basis[32:, shared:])], axis=1)
         rz_part = row_sum(half_sol * res_ref[...])
 
         if not last:
             @pl.when(step == 0)
             def _():
+                turn(1, 0, shared)
                 settle(stiff_hi, stiff_lo, 0, shared, 0, ndof // tall)
 
         precond = add_faces(half_sol, wait_faces(0))
@@ -313,31 +323,42 @@
         zz_part = row_sum(precond * image)
         zq_part = row_sum(weight * precond * image_ref[...])
         start_sums(now, [rz_part, zz_part, zq_part])
-        image = add_faces(image, wait_faces(1))
-        if not last:
-            start_gather(later, image)
+        if last:
+            kept = unturn(sol_ref[...], precond) + unturn(direction_ref[...], res_ref[...])
+            image = add_faces(image, wait_faces(1))
+        else:
+            coarse_own = coarse_of(weight * image)
+            incoming = wait_faces(1)
+            coarse_near = coarse_of(0.5 * incoming)
+            start_gather(later, coarse_own + coarse_near)
+            image = add_faces(image, incoming)
         lift_sums(now)
-        if not last:
+        if last:
+            kept = kept + unturn(image, image_ref[...])
+        else:
             start_spread(later)
         rz, zz, zq = wait_sums(now)
         beta = jnp.where(step > 0, rz / scalars[0:1], 0.0)
         denom = zz + beta * (2.0 * zq) + beta * (beta * jnp.where(step > 0, scalars[1:2], 0.0))
         alpha = rz / denom
         slope, length = as_column(beta), as_column(alpha)
+        if last:
+            sol_out[...] = kept[0] + length * (kept[1] + slope * kept[2])
+            res_out[...] = kept[3] - length * (kept[4] + slope * kept[5])
+            return
         direction = precond + slope * direction_ref[...]
         image = image + slope * image_ref[...]
         resid = res_ref[...] - length * image
         sol_ref[...] = sol_ref[...] + length * direction
         res_ref[...] = resid
-        if not last:
-            direction_ref[...] = direction
-            image_ref[...] = image
-            scalars[0:1] = rz
-            scalars[1:2] = denom
-            local_ref[...] = product(weight * resid, neum_hi, neum_lo, 0, ndof)
-            coarse_image = wait_spread(later) + beta * coarse_state[1]
-            coarse_state[1] = coarse_image
-            coarse_state[0] = coarse_state[0] - alpha * coarse_image
+        direction_ref[...] = direction
+        image_ref[...] = image
+        scalars[0:1] = rz
+        scalars[1:2] = denom
+        local_ref[...] = product(weight * resid, neum_hi, neum_lo, 0, ndof)
+        coarse_image = wait_spread(later) + beta * coarse_state[1]
+        coarse_state[1] = coarse_image
+        coarse_state[0] = coarse_state[0] - alpha * coarse_image
 
     def body(step, carry):
         iterate(step, False)
@@ -345,8 +366,11 @@
 
     lax.fori_loop(0, ITERS - 1, body, 0)
     iterate(ITERS - 1, True)
-    sol_out[0] = three(dot(jnp.concatenate(thirds(sol_ref[...]), axis=0), perm[...]), cases)
-    res_out[0] = three(dot(jnp.concatenate(thirds(res_ref[...]), axis=0), perm[...]), cases)
+
+
+def hand_over(sol_ref, res_ref, sol_out, res_out):
+    sol_out[0] = sol_ref[...]
+    res_out[0] = res_ref[...]
 
 
 def local(sizes, cycle, stiffness, neumann_inv, coarse_basis, coarse_inv, loads, face_index, face_len):
@@ -359,9 +383,10 @@
     square = pltpu.VMEM((ndof, ndof), BF16)
     plain = pltpu.VMEM((cases, ndof), F32)
     whole = jax.ShapeDtypeStruct((1, cases, ndof), F32)
-    return pl.pallas_call(
+    flat = jax.ShapeDtypeStruct((cases, ndof), F32)
+    results = pl.pallas_call(
         functools.partial(kernel, sizes, cycle),
-        out_shape=(whole, whole),
+        out_shape=(flat, flat),
         in_specs=[anywhere, anywhere, inside, anywhere, inside, inside, pl.BlockSpec(memory_space=pltpu.SMEM)],
         out_specs=(inside, inside),
         scratch_shapes=[
@@ -399,6 +424,9 @@
         ),
         name="solve",
     )(stiffness, neumann_inv, coarse_basis, coarse_inv, loads, face_index, face_len)
+    return pl.pallas_call(
+        hand_over, out_shape=(whole, whole), in_specs=[inside] * 2, out_specs=(inside, inside), name="hand_over"
+    )(*results)
 
 
 def solution(mesh, plane=PLANE, cycle=CYCLE):

time: 118 us -> 119 us (level)
  Pallas kernels: 114 us -> 118 us
  local copies, waits for them, and re-layouts: 3.34 us -> 0 us
    pallas_call x1 -> x2, Pallas kernels: 114 us -> 118 us  [the longest x1 116 us: local(): pl.pallas_call(functools.partial(kernel, sizes, cycle), out_shape=(flat,...]
    unnamed x2 -> x0, local copies, waits for them, and re-layouts: 3.34 us -> none
where the time goes in v4:
time: 119 us
  Pallas kernels  118 us (99%)
    pallas_call x1, Pallas kernels, local(): pl.pallas_call(functools.partial(kernel, sizes, cycle), out_shape=(flat,...  116 us

profile of v4, /device:TPU:1, one launch (start us, length us, event | category | flops | bytes accessed | tf_op | source)
XLA Modules:
  0.0 118.5 jit_solution(1847072735032831429)
XLA Ops:
  0.6 116.0 %solve.1 = (f32[64,1024]{1,0:T(8,128)}, f32[64,1024]{1,0:T(8,128)}) custom-call(f32[1,1024,1024]{2,1,0:T(8,128)} %stiff_hbm.1, f32[1,1024,1024]{2,1,0:T(8,128)} %neum_hbm.1, f32[1,16,1024]{2,1,0:T(8,128)} %basis_ref.1, f32[16,4096]{1,0:T(8,128)} %coarse_hbm.1, f32[1,64,1024]{2,1,0:T(8,128)} %loads_ref.1, s32[1,4,128]{2,1,0:T(4,128)} %index_ref.1, s32[1,4]{1,0:T(1,128)} %len_ref.1), custom_call_target="tpu_custom_call" | custom-call | tf_op jit(solution)/shard_map/solve/pallas_call | solution.py:387
  116.7 1.8 %hand_over.1 = (f32[1,64,1024]{2,1,0:T(8,128)}, f32[1,64,1024]{2,1,0:T(8,128)}) custom-call(f32[64,1024]{1,0:T(8,128)} %get-tuple-element.4.sol_ref, f32[64,1024]{1,0:T(8,128)} %get-tuple-element.5.res_ref), custom_call_target="tpu_custom_call" | custom-call | tf_op jit(solution)/shard_map/hand_over/pallas_call | solution.py:427

commit v5 on v4

--- a/solution.py
+++ b/solution.py
@@ -48,7 +48,8 @@
     raw, perm, turned_hi, turned_lo, neum_hi, neum_lo, stiff_hi, stiff_lo, basis, sol_ref, res_ref,
     coarse_raw, coarse_cat, image_ref, direction_ref, local_ref, scalars, coarse_state, face_out, face_in,
     gather, gather_own, spread, spread_out, sums, sums_own, tops, tops_own,
-    load_sem, face_send, face_recv, flat_send, flat_recv, deep_send, deep_recv,
+    side_basis, side_mix, side_wide, side_out, side_in,
+    load_sem, face_send, face_recv, side_send, side_recv, flat_send, flat_recv, deep_send, deep_recv,
 ):
     planes, plane = sizes
     subs = planes * plane
@@ -67,8 +68,22 @@
         lax.rem(me + subs - 1, subs), lax.rem(me + 1, subs),
         lax.rem(me + subs - cycle, subs), lax.rem(me + cycle, subs),
     )
-    flat_others = [(me - col + at, at) for at in [lax.rem(col + step, plane) for step in range(1, plane)]]
-    deep_others = [(me + (at - deep) * plane, at) for at in [lax.rem(deep + step, planes) for step in range(1, planes)]]
+    span = min(4, plane // 2)
+    tall_y = plane // (2 * span)
+    at_y, at_x, at_core = col // (2 * span), lax.rem(col // 2, span), lax.rem(col, 2)
+
+    def hops(step, length):
+        return min(step, length - step)
+
+    offsets = [(y, x, c) for y in range(tall_y) for x in range(span) for c in range(2)][1:]
+    offsets.sort(key=lambda d: -hops(d[0], tall_y) - hops(d[1], span))
+    flat_places = [
+        lax.rem(at_y + y, tall_y) * (2 * span) + lax.rem(at_x + x, span) * 2 + lax.rem(at_core + c, 2)
+        for y, x, c in offsets
+    ]
+    deep_steps = sorted(range(1, planes), key=lambda step: -hops(step, planes))
+    flat_others = [(me - col + at, at) for at in flat_places]
+    deep_others = [(me + (at - deep) * plane, at) for at in [lax.rem(deep + step, planes) for step in deep_steps]]
 
     def remote(src, dst, send, recv, peer):
         return pltpu.make_async_remote_copy(
@@ -121,6 +136,24 @@
         got = jnp.concatenate([face_in[kind, block] for block in range(faces)], axis=1)
         return jnp.where(live, got, 0.0)
 
+    def side_copy(kind, block):
+        pair = block ^ 1
+        source, target = (
+            (side_basis.at[0, block], side_basis.at[1, pair]) if kind == 2
+            else (side_out.at[kind, block], side_in.at[kind, pair])
+        )
+        return remote(source, target, side_send.at[kind, block], side_recv.at[kind, pair], sides[block])
+
+    def start_sides(kind):
+        for block in range(faces):
+            side_copy(kind, block).start()
+
+    def wait_sides(kind):
+        for block in range(faces):
+            side_copy(kind, block).wait_send()
+        for block in range(faces):
+            side_copy(kind, block).wait_recv()
+
     def add_faces(value, incoming):
         return jnp.concatenate([value[:, :shared] + incoming, value[:, shared:]], axis=1)
 
@@ -145,25 +178,29 @@
         for copy in push(*args):
             copy.start()
 
-    def wait_all(kind, turn, others, src_of, dst, send, recv):
-        for copy in pull(kind, turn, others, src_of, dst, send, recv):
+    def wait_received(*args):
+        for copy in pull(*args):
+            copy.wait_recv()
+
+    def wait_sent(*args):
+        for copy in pull(*args):
             copy.wait_send()
-        for copy in pull(kind, turn, others, src_of, dst, send, recv):
-            copy.wait_recv()
 
     def coarse_of(scaled):
         high, low = halves(scaled)
         return dot_nt(basis[:32, :scaled.shape[1]], jnp.concatenate([high, low], axis=0))
 
-    def start_gather(turn, out):
+    def pack(out):
         value = out[:16] + flip(out[:16]) + out[16:]
-        own = jnp.where(left_half, value[:8], flip(value[8:]))
+        return jnp.where(left_half, value[:8], flip(value[8:]))
+
+    def start_gather(turn, own):
         gather_own[...] = own
         gather[turn, col] = own
         start_all(0, turn, flat_others, lambda at: gather_own, gather, col, flat_send, flat_recv)
 
     def start_spread(turn):
-        wait_all(0, turn, flat_others, lambda at: gather_own, gather, flat_send, flat_recv)
+        wait_received(0, turn, flat_others, lambda at: gather_own, gather, flat_send, flat_recv)
         packed = gather[turn]
         turned = flip(packed)
         both = jnp.concatenate(
@@ -178,16 +215,20 @@
         spread_out[...] = jnp.where(left_half, value[:, 0], flip(value[:, 1]))
         spread[turn, deep] = spread_out[deep]
         start_all(0, turn, deep_others, lambda at: spread_out.at[at], spread, deep, deep_send, deep_recv)
+        wait_sent(0, turn, flat_others, lambda at: gather_own, gather, flat_send, flat_recv)
 
     def wait_spread(turn):
-        wait_all(0, turn, deep_others, lambda at: spread_out.at[at], spread, deep_send, deep_recv)
+        wait_sent(0, turn, deep_others, lambda at: spread_out.at[at], spread, deep_send, deep_recv)
+        wait_received(0, turn, deep_others, lambda at: spread_out.at[at], spread, deep_send, deep_recv)
         return jnp.sum(spread[turn], axis=0)
 
-    def coarse_rows(packed):
+    def coarse_stack(packed):
         both = jnp.concatenate([packed, flip(packed)], axis=0)
         high = both.astype(BF16).astype(F32)
-        stacked = jnp.concatenate([high, high, both - high, jnp.zeros_like(high)], axis=0)
-        return stacked.T[:cases].astype(BF16)
+        return jnp.concatenate([high, high, both - high, jnp.zeros_like(high)], axis=0)
+
+    def coarse_rows(*packed):
+        return jnp.concatenate([coarse_stack(one) for one in packed], axis=0).T[:cases].astype(BF16)
 
     def row_sum(value):
         part = value[:, :128]
@@ -206,14 +247,16 @@
         start_all(1, turn, flat_others, lambda at: sums_own, sums, col, flat_send, flat_recv)
 
     def lift_sums(turn):
-        wait_all(1, turn, flat_others, lambda at: sums_own, sums, flat_send, flat_recv)
+        wait_received(1, turn, flat_others, lambda at: sums_own, sums, flat_send, flat_recv)
         own = jnp.sum(sums[turn], axis=0)
         tops_own[...] = own
         tops[turn, deep] = own
         start_all(1, turn, deep_others, lambda at: tops_own, tops, deep, deep_send, deep_recv)
+        wait_sent(1, turn, flat_others, lambda at: sums_own, sums, flat_send, flat_recv)
 
     def wait_sums(turn):
-        wait_all(1, turn, deep_others, lambda at: tops_own, tops, deep_send, deep_recv)
+        wait_sent(1, turn, deep_others, lambda at: tops_own, tops, deep_send, deep_recv)
+        wait_received(1, turn, deep_others, lambda at: tops_own, tops, deep_send, deep_recv)
         total = jnp.sum(tops[turn], axis=0)
         return total[:, :wide], total[:, wide:2 * wide], total[:, 2 * wide:]
 
@@ -261,14 +304,20 @@
         hit = place == iota((128, ndof), 0) + block
         perm[shared + block:shared + block + 128, :] = jnp.where(hit, 1.0, 0.0).astype(BF16)
     rest = three(dot_nt(loads_cat, perm[shared:, :]), cases)
-    basis_hi, basis_lo = halves(three(dot_nt(jnp.concatenate(thirds(basis_ref[0]), axis=0), perm[...]), 16))
+    basis_own = three(dot_nt(jnp.concatenate(thirds(basis_ref[0]), axis=0), perm[...]), 16)
+    for block in range(faces):
+        side_basis[0, block] = basis_own[:, block * width:(block + 1) * width]
+    start_sides(2)
+    side_mix[...] = jnp.zeros_like(side_mix)
+    side_wide[...] = jnp.zeros_like(side_wide)
+    basis_hi, basis_lo = halves(basis_own)
     basis[...] = jnp.concatenate(
         [basis_hi, basis_lo, basis_hi, basis_lo, basis_hi, jnp.zeros_like(basis_hi)], axis=0
     )
     load_neum.wait()
-    turn(0, 0, shared)
+    turn(0, 0, ndof)
     resid = jnp.concatenate([first + wait_faces(1), rest], axis=1)
-    start_gather(0, coarse_of(weight * resid))
+    start_gather(0, pack(coarse_of(weight * resid)))
     res_ref[...] = resid
     load_coarse.wait()
     for receive in (False, True):
@@ -282,13 +331,24 @@
                 copy.wait_send()
     coarse_hi, coarse_lo = halves(coarse_raw[...].reshape(planes * 16, plane * 16))
     coarse_cat[...] = jnp.concatenate([coarse_hi, coarse_lo], axis=0)
-    turn(0, shared, ndof)
-    settle(neum_hi, neum_lo, 0, shared, 0, ndof // tall)
+    settle(neum_hi, neum_lo, 0, ndof, 0, ndof // tall)
     start_spread(0)
-    settle(neum_hi, neum_lo, shared, ndof, 0, ndof // tall)
     local_ref[...] = product(weight * res_ref[...], neum_hi, neum_lo, 0, ndof)
+    start_faces(0, weight[:, :shared] * local_ref[:, :shared])
+    wait_sides(2)
+    for block in range(faces):
+        near_basis = side_basis[1, block] * jnp.where(live[:, block * width:(block + 1) * width], 0.5, 0.0)
+        high, low = halves(near_basis)
+        at = slice(block * width, (block + 1) * width)
+        side_mix[32 * block:32 * (block + 1), at] = jnp.concatenate([high, low], axis=0)
+        side_wide[64 * block:64 * (block + 1), at] = jnp.concatenate([high, low, high, jnp.zeros_like(high)], axis=0)
     load_stiff.wait()
-    coarse_state[0] = wait_spread(0)
+    turn(1, 0, shared)
+    coarse_first = wait_spread(0)
+    coarse_state[0] = coarse_first
+    for block in range(faces):
+        side_out[0, block] = coarse_first
+    start_sides(0)
     coarse_state[1] = jnp.zeros_like(coarse_state[1])
 
     def unturn(one, two):
@@ -298,19 +358,25 @@
     def iterate(step, last):
         now, later = (step % 2, (step + 1) % 2) if last else (lax.rem(step, 2), lax.rem(step + 1, 2))
         coarse_part = coarse_rows(coarse_state[0])
-        near_sol = weight[:, :shared] * (local_ref[:, :shared] + dot(coarse_part, basis[32:, :shared]))
-        start_faces(0, near_sol)
-        half_sol = jnp.concatenate([near_sol, local_ref[:, shared:] + dot(coarse_part, basis[32:, shared:])], axis=1)
+        half_sol = weight * (local_ref[...] + dot(coarse_part, basis[32:, :]))
         rz_part = row_sum(half_sol * res_ref[...])
 
         if not last:
             @pl.when(step == 0)
             def _():
-                turn(1, 0, shared)
                 settle(stiff_hi, stiff_lo, 0, shared, 0, ndof // tall)
 
-        precond = add_faces(half_sol, wait_faces(0))
+        incoming = wait_faces(0)
+        wait_sides(0)
+        incoming = incoming + dot(coarse_rows(*[side_in[0, block] for block in range(faces)]), side_wide[...])
+        precond = add_faces(half_sol, incoming)
         near = product(precond, stiff_hi, stiff_lo, 0, shared)
+        if not last:
+            high, low = halves(near)
+            mixed = dot_nt(side_mix[...], jnp.concatenate([high, low], axis=0))
+            for block in range(faces):
+                side_out[1, block] = pack(mixed[32 * block:32 * (block + 1)])
+            start_sides(1)
         start_faces(1, near)
 
         if not last:
@@ -327,11 +393,10 @@
             kept = unturn(sol_ref[...], precond) + unturn(direction_ref[...], res_ref[...])
             image = add_faces(image, wait_faces(1))
         else:
-            coarse_own = coarse_of(weight * image)
-            incoming = wait_faces(1)
-            coarse_near = coarse_of(0.5 * incoming)
-            start_gather(later, coarse_own + coarse_near)
-            image = add_faces(image, incoming)
+            coarse_own = pack(coarse_of(weight * image))
+            wait_sides(1)
+            start_gather(later, coarse_own + jnp.sum(side_in[1], axis=0))
+            image = add_faces(image, wait_faces(1))
         lift_sums(now)
         if last:
             kept = kept + unturn(image, image_ref[...])
@@ -355,10 +420,16 @@
         image_ref[...] = image
         scalars[0:1] = rz
         scalars[1:2] = denom
-        local_ref[...] = product(weight * resid, neum_hi, neum_lo, 0, ndof)
+        local_next = product(weight * resid, neum_hi, neum_lo, 0, ndof)
+        start_faces(0, weight[:, :shared] * local_next[:, :shared])
+        local_ref[...] = local_next
         coarse_image = wait_spread(later) + beta * coarse_state[1]
+        coarse_next = coarse_state[0] - alpha * coarse_image
+        for block in range(faces):
+            side_out[0, block] = coarse_next
+        start_sides(0)
         coarse_state[1] = coarse_image
-        coarse_state[0] = coarse_state[0] - alpha * coarse_image
+        coarse_state[0] = coarse_next
 
     def body(step, carry):
         iterate(step, False)
@@ -411,9 +482,16 @@
             pltpu.VMEM((1, 3 * wide), F32),
             pltpu.VMEM((2, planes, 1, 3 * wide), F32),
             pltpu.VMEM((1, 3 * wide), F32),
+            pltpu.VMEM((2, faces, 16, width), F32),
+            pltpu.VMEM((32 * faces, faces * width), BF16),
+            pltpu.VMEM((64 * faces, faces * width), BF16),
+            pltpu.VMEM((2, faces, 8, wide), F32),
+            pltpu.VMEM((2, faces, 8, wide), F32),
             pltpu.SemaphoreType.DMA((3,)),
             pltpu.SemaphoreType.DMA((2, faces)),
             pltpu.SemaphoreType.DMA((2, faces)),
+            pltpu.SemaphoreType.DMA((3, faces)),
+            pltpu.SemaphoreType.DMA((3, faces)),
             pltpu.SemaphoreType.DMA((2, 2, plane)),
             pltpu.SemaphoreType.DMA((2, 2, plane)),
             pltpu.SemaphoreType.DMA((3, 2, planes)),

time: 119 us -> 113 us (0.950)
  Pallas kernels: 118 us -> 112 us
    pallas_call x1, Pallas kernels: 116 us -> 110 us  [local(): pl.pallas_call(functools.partial(kernel, sizes, cycle), out_shape=(flat,...]
where the time goes in v5:
time: 113 us
  Pallas kernels  112 us (99%)
    pallas_call x1, Pallas kernels, local(): pl.pallas_call(functools.partial(kernel, sizes, cycle), out_shape=(flat,...  110 us

profile of v5, /device:TPU:1, one launch (start us, length us, event | category | flops | bytes accessed | tf_op | source)
XLA Modules:
  0.0 112.5 jit_solution(13571436728363450828)
XLA Ops:
  0.6 110.0 %solve.1 = (f32[64,1024]{1,0:T(8,128)}, f32[64,1024]{1,0:T(8,128)}) custom-call(f32[1,1024,1024]{2,1,0:T(8,128)} %stiff_hbm.1, f32[1,1024,1024]{2,1,0:T(8,128)} %neum_hbm.1, f32[1,16,1024]{2,1,0:T(8,128)} %basis_ref.1, f32[16,4096]{1,0:T(8,128)} %coarse_hbm.1, f32[1,64,1024]{2,1,0:T(8,128)} %loads_ref.1, s32[1,4,128]{2,1,0:T(4,128)} %index_ref.1, s32[1,4]{1,0:T(1,128)} %len_ref.1), custom_call_target="tpu_custom_call" | custom-call | tf_op jit(solution)/shard_map/solve/pallas_call | solution.py:458
  110.7 1.8 %hand_over.1 = (f32[1,64,1024]{2,1,0:T(8,128)}, f32[1,64,1024]{2,1,0:T(8,128)}) custom-call(f32[64,1024]{1,0:T(8,128)} %get-tuple-element.4.sol_ref, f32[64,1024]{1,0:T(8,128)} %get-tuple-element.5.res_ref), custom_call_target="tpu_custom_call" | custom-call | tf_op jit(solution)/shard_map/hand_over/pallas_call | solution.py:505

commit v6 on v5

--- a/solution.py
+++ b/solution.py
@@ -46,7 +46,7 @@
 def kernel(
     sizes, cycle, stiff_hbm, neum_hbm, basis_ref, coarse_hbm, loads_ref, index_ref, len_ref, sol_out, res_out,
     raw, perm, turned_hi, turned_lo, neum_hi, neum_lo, stiff_hi, stiff_lo, basis, sol_ref, res_ref,
-    coarse_raw, coarse_cat, image_ref, direction_ref, local_ref, scalars, coarse_state, face_out, face_in,
+    coarse_raw, coarse_cat, image_ref, direction_ref, local_ref, slope_ref, edge_ref, scalars, coarse_state, face_out, face_in,
     gather, gather_own, spread, spread_out, sums, sums_own, tops, tops_own,
     side_basis, side_mix, side_wide, side_out, side_in,
     load_sem, face_send, face_recv, side_send, side_recv, flat_send, flat_recv, deep_send, deep_recv,
@@ -350,6 +350,9 @@
         side_out[0, block] = coarse_first
     start_sides(0)
     coarse_state[1] = jnp.zeros_like(coarse_state[1])
+    slope_ref[...] = jnp.zeros_like(slope_ref)
+    edge_ref[0] = wait_faces(0)
+    edge_ref[1] = jnp.zeros_like(edge_ref[1])
 
     def unturn(one, two):
         both = three(dot(jnp.concatenate(thirds(jnp.concatenate([one, two], axis=0)), axis=0), perm[...]), 2 * cases)
@@ -366,9 +369,8 @@
             def _():
                 settle(stiff_hi, stiff_lo, 0, shared, 0, ndof // tall)
 
-        incoming = wait_faces(0)
         wait_sides(0)
-        incoming = incoming + dot(coarse_rows(*[side_in[0, block] for block in range(faces)]), side_wide[...])
+        incoming = edge_ref[0] + dot(coarse_rows(*[side_in[0, block] for block in range(faces)]), side_wide[...])
         precond = add_faces(half_sol, incoming)
         near = product(precond, stiff_hi, stiff_lo, 0, shared)
         if not last:
@@ -397,6 +399,8 @@
             wait_sides(1)
             start_gather(later, coarse_own + jnp.sum(side_in[1], axis=0))
             image = add_faces(image, wait_faces(1))
+            local_image = product(weight * image, neum_hi, neum_lo, 0, ndof)
+            start_faces(0, weight[:, :shared] * local_image[:, :shared])
         lift_sums(now)
         if last:
             kept = kept + unturn(image, image_ref[...])
@@ -420,9 +424,12 @@
         image_ref[...] = image
         scalars[0:1] = rz
         scalars[1:2] = denom
-        local_next = product(weight * resid, neum_hi, neum_lo, 0, ndof)
-        start_faces(0, weight[:, :shared] * local_next[:, :shared])
-        local_ref[...] = local_next
+        local_image = local_image + slope * slope_ref[...]
+        slope_ref[...] = local_image
+        local_ref[...] = local_ref[...] - length * local_image
+        edge_image = wait_faces(0) + slope * edge_ref[1]
+        edge_ref[1] = edge_image
+        edge_ref[0] = edge_ref[0] - length * edge_image
         coarse_image = wait_spread(later) + beta * coarse_state[1]
         coarse_next = coarse_state[0] - alpha * coarse_image
         for block in range(faces):
@@ -470,6 +477,8 @@
             pltpu.VMEM((cases, ndof), F32),
             pltpu.VMEM((cases, ndof), F32),
             pltpu.VMEM((cases, ndof), F32),
+            plain,
+            pltpu.VMEM((2, cases, faces * width), F32),
             pltpu.VMEM((8, wide), F32),
             pltpu.VMEM((2, 8, wide), F32),
             pltpu.VMEM((2, faces, cases, width), F32),

time: 113 us -> 113 us (level)
  no operation moved by 1% of the time
where the time goes in v6:
time: 113 us; the launch traced here: 112 us
  Pallas kernels  112 us (99%)
    pallas_call x1, Pallas kernels, local(): pl.pallas_call(functools.partial(kernel, sizes, cycle), out_shape=(flat,...  110 us

profile of v6, /device:TPU:1, one launch (start us, length us, event | category | flops | bytes accessed | tf_op | source)
XLA Modules:
  0.0 112.4 jit_solution(7435054656180886734)
XLA Ops:
  0.6 109.9 %solve.1 = (f32[64,1024]{1,0:T(8,128)}, f32[64,1024]{1,0:T(8,128)}) custom-call(f32[1,1024,1024]{2,1,0:T(8,128)} %stiff_hbm.1, f32[1,1024,1024]{2,1,0:T(8,128)} %neum_hbm.1, f32[1,16,1024]{2,1,0:T(8,128)} %basis_ref.1, f32[16,4096]{1,0:T(8,128)} %coarse_hbm.1, f32[1,64,1024]{2,1,0:T(8,128)} %loads_ref.1, s32[1,4,128]{2,1,0:T(4,128)} %index_ref.1, s32[1,4]{1,0:T(1,128)} %len_ref.1), custom_call_target="tpu_custom_call" | custom-call | tf_op jit(solution)/shard_map/solve/pallas_call | solution.py:465
  110.6 1.8 %hand_over.1 = (f32[1,64,1024]{2,1,0:T(8,128)}, f32[1,64,1024]{2,1,0:T(8,128)}) custom-call(f32[64,1024]{1,0:T(8,128)} %get-tuple-element.4.sol_ref, f32[64,1024]{1,0:T(8,128)} %get-tuple-element.5.res_ref), custom_call_target="tpu_custom_call" | custom-call | tf_op jit(solution)/shard_map/hand_over/pallas_call | solution.py:514
